TPU v7x, 128 devices: a whole 4x4x4 slice. The times are simulated.
128 devices in a mesh: alpha: 8 (over x, core), beta: 16 (over z, y).
Axes of the slice: x: 4, y: 4, z: 4, core: 2. Of those that a mesh axis runs over, the one named last changes fastest.
Arguments:
- csf_coef: float32 [42, 98304], P(None, ('alpha', 'beta')), may hold values from -18 to 18
- conf_class: int32 [98304], P(('alpha', 'beta')), may hold values from 0 to 5
- conf_tile: int32 [98304, 1], P(('alpha', 'beta')), may hold values from 0 to 127, as said below
- transforms: float32 [6, 42, 256], replicated, may hold values from -1 to 1
- alpha_targets: int32 [16, 12288], P(None, 'alpha'), may hold values from 0 to 12287, as said below
- alpha_values: bfloat16 [16, 12288], P(None, 'alpha'), may hold values from -1.796875 to 1.796875
- alpha_counts: int32 [12288], P('alpha'), may hold values from 1 to 16, as said below
- beta_targets: int32 [16, 6144], P(None, 'beta'), may hold values from 0 to 6143, as said below
- beta_values: bfloat16 [16, 6144], P(None, 'beta'), may hold values from -1.796875 to 1.796875
- beta_counts: int32 [6144], P('beta'), may hold values from 1 to 16, as said below
- det_diag: float32 [12288, 6144], P('alpha', 'beta'), may hold values from 0.5 to 2
Outputs:
- residual: float32 [42, 98304], P(None, ('alpha', 'beta'))
- residual_rms: float32 [], replicated
Inputs may be any that keep to these rules, and one draw needn't show every extreme that they name: `conf_tile`: among the 768 configurations of one device no tile is named more than 18 times; in every draw some tile is named exactly 18 times by the configurations of every device. `alpha_targets`: in each column the 16 entries are distinct and differ from the column's own string. `beta_targets`: in each column the 16 entries are distinct and differ from the column's own string. `alpha_counts`: some string has exactly 16. `beta_counts`: some string has exactly 16.
All inputs are finite; a program needn't handle non-finite values.
Results may differ from a plain program's by a relative error of at most 0.00075.
The roundings to bfloat16 on the way count: a program that leaves them out, or rounds other values in their place, can miss the bound.
Values may be sent and summed in bfloat16 or wider, within the bound.
No kernel may reach another device: no remote copies, remote signals or barrier semaphores. Data moves between devices by JAX's collectives and lax.ppermute only.
A program may use at most 128 MiB of HBM per device.

v0:
```python
import functools

import jax
import jax.numpy as jnp
from jax import lax
from jax.experimental import pallas as pl
from jax.experimental.pallas import tpu as pltpu
from jax.sharding import PartitionSpec as P


F32 = jnp.float32
BF16 = jnp.bfloat16
HIGH = lax.Precision.HIGHEST
BOTH = ("alpha", "beta")
PAD = 8
FIRST = 4
STEPS = 2
VMEM_LIMIT = 60 * 1024 * 1024


def stacked(coef, classes, classes_n):
    parts = []
    for c in range(classes_n):
        parts.append(jnp.where(classes == c, coef, jnp.zeros_like(coef)))
    return jnp.concatenate(parts, axis=0)


def padded(ref, index=None):
    value = ref[...] if index is None else ref[index]
    fill = -value.shape[0] % 8
    return jnp.concatenate([value, jnp.zeros((fill, value.shape[1]), F32)], axis=0)


def pack_kernel(capacity, coef_ref, label_ref, tr_ref, out_ref, key_ref, inter_ref):
    confs = coef_ref.shape[1]
    ncls = tr_ref.shape[0]
    devices = confs * 3 // capacity
    masked = stacked(padded(coef_ref), label_ref[0:1, :], ncls)
    trans = jnp.concatenate([padded(tr_ref, c) for c in range(ncls)], axis=0)
    dets = lax.dot_general(
        masked, trans, (((0,), (0,)), ((), ())), precision=HIGH, preferred_element_type=F32
    ).astype(BF16)
    tile = label_ref[1:2, :]
    hit = lax.broadcasted_iota(jnp.int32, (devices, confs), 0) == tile
    before = lax.broadcasted_iota(jnp.int32, (confs, confs), 0) < lax.broadcasted_iota(
        jnp.int32, (confs, confs), 1
    )
    counts = jnp.dot(
        hit.astype(F32).astype(BF16), before.astype(F32).astype(BF16), preferred_element_type=F32
    )
    slot = jnp.sum(jnp.where(hit, counts, 0.0), axis=0, keepdims=True).astype(jnp.int32)
    key = tile * capacity + slot
    key_ref[...] = key
    rows = devices * capacity
    block = 256
    for b in range(rows // block):
        onehot = (
            (lax.broadcasted_iota(jnp.int32, (block, confs), 0) + b * block == key)
            .astype(F32)
            .astype(BF16)
        )
        picked = jnp.dot(onehot, dets, preferred_element_type=F32)
        for h in range(2):
            inter_ref[pl.ds(h, block, stride=2), :] = picked[:, h * 128 : (h + 1) * 128]
        out_ref[pl.ds(b * 2 * block, 2 * block), :] = inter_ref[...].astype(BF16)


def pack(coef, labels, transforms, capacity):
    confs = coef.shape[1]
    rows = 2 * 3 * confs
    return pl.pallas_call(
        functools.partial(pack_kernel, capacity),
        out_shape=(
            jax.ShapeDtypeStruct((rows, 128), BF16),
            jax.ShapeDtypeStruct((1, confs), jnp.int32),
        ),
        scratch_shapes=[pltpu.VMEM((512, 128), F32)],
        compiler_params=pltpu.CompilerParams(vmem_limit_bytes=VMEM_LIMIT),
        name="pack",
    )(coef, labels, transforms)


def build_table(x_ref, table_ref, stage_ref):
    blocks, rows, _ = x_ref.shape
    lanes = rows // 3

    def build(j, carry):
        stage_ref[...] = x_ref[j].astype(F32)
        for ct in range(3):
            piece = stage_ref[pl.ds(ct, lanes, stride=3), :]
            piece = jnp.concatenate([piece, jnp.zeros((128 - lanes, 128), F32)], axis=0)
            start = pl.multiple_of((j * 3 + ct) * 128 + PAD, 8)
            table_ref[pl.ds(start, 128), :] = piece.T
        return carry

    lax.fori_loop(0, blocks, build, 0)


def plan_kernel(steps, tgt_ref, val_ref, cnt_ref, out_ref):
    exc, length = tgt_ref.shape
    counts = cnt_ref[...]
    place = lax.broadcasted_iota(jnp.int32, (1, length), 1)
    key = counts * 4096 + (4095 - place)
    key8 = jnp.broadcast_to(key, (8, length)).astype(F32)
    slots = lax.broadcasted_iota(jnp.int32, (exc, length), 0)
    live = jnp.where(slots < counts, val_ref[...].astype(F32), 0.0)
    tgt = tgt_ref[...]
    high = tgt >> 7
    rows = lax.broadcasted_iota(jnp.int32, (8, length), 0)
    extra = jnp.where(rows == 0, place >> 7, jnp.where(rows == 1, place & 127, 0))
    lists = jnp.concatenate(
        [high.astype(F32), (tgt & 127).astype(F32), live, extra.astype(F32)], axis=0
    ).astype(BF16)
    total = jnp.zeros((lists.shape[0], length), F32)
    for k in range(length // 128):
        mine = key8[:, k * 128 : (k + 1) * 128]
        column = jnp.concatenate([mine] * 16, axis=0).T[:, 0:1]
        ahead = jnp.where(key8[0:1, :] > column, 1.0, 0.0)
        rank = jnp.sum(ahead, axis=1, keepdims=True).astype(jnp.int32)
        moved = (
            (lax.broadcasted_iota(jnp.int32, (128, length), 1) == rank).astype(F32).astype(BF16)
        )
        total = total + jnp.dot(
            lists[:, k * 128 : (k + 1) * 128], moved, preferred_element_type=F32
        )
    lane = lax.broadcasted_iota(jnp.int32, (8, length), 1)
    bounds = jnp.zeros((8, length), F32)
    for k in range(exc // steps):
        over = jnp.sum(jnp.where(counts > k * steps, 1.0, 0.0), axis=1, keepdims=True)
        groups = ((over.astype(jnp.int32) + 7) >> 3).astype(F32)
        bounds = jnp.where(jnp.logical_and(lane == k, rows == 2), groups, bounds)
    out_ref[0 : 3 * exc, :] = total[: 3 * exc]
    out_ref[3 * exc :, :] = jnp.where(rows == 2, bounds, total[3 * exc :])


def plan(targets, values, counts, steps):
    exc, length = targets.shape
    return pl.pallas_call(
        functools.partial(plan_kernel, steps),
        out_shape=jax.ShapeDtypeStruct((3 * exc + 8, length), F32),
        compiler_params=pltpu.CompilerParams(vmem_limit_bytes=VMEM_LIMIT),
        name="plan",
    )(targets, values, counts[None, :])


def beta_block(table_ref, tgt_ref, row_ref, w_ref, out_ref, wt_ref, acc_ref):
    lanes = out_ref.shape[1] // 3
    exc = 16
    cols = 384
    sub = lax.broadcasted_iota(jnp.int32, (8, 128), 0)
    for ct in range(3):
        wt_ref[pl.ds(ct * 128, 128), :] = jnp.concatenate(
            [w_ref[0, pl.ds(ct, exc, stride=3), :], jnp.zeros((128 - exc, 128), F32)], axis=0
        ).T
    buckets = exc // STEPS
    at = (exc + 1) * cols

    def make(depth):
        def group(g, carry):
            first = pl.multiple_of(g * 8, 8)
            near = tgt_ref.at[pl.ds(first, exc * cols)]
            w8 = wt_ref[pl.ds(first, 8), :]
            acc = jnp.zeros((8, 128), F32)
            for e in range(depth):
                got = None
                for s in range(8):
                    t = near[e * cols + s]
                    win = table_ref[pl.ds(t + (PAD - s), 8), :]
                    got = win if s == 0 else jnp.where(sub == s, win, got)
                acc = acc + got * w8[:, e : e + 1]
            acc_ref[pl.ds(first, 8), :] = acc
            return carry

        return group

    for k in reversed(range(buckets)):
        begin = tgt_ref[at + k + 1] if k + 1 < buckets else 0
        lax.fori_loop(begin, tgt_ref[at + k], make((k + 1) * STEPS), 0)
    ids = jnp.concatenate([row_ref[0, exc * 3 + ct : exc * 3 + ct + 1, :] for ct in range(3)], axis=1)
    back = (
        (lax.broadcasted_iota(jnp.int32, (cols, cols), 0) == ids).astype(F32).astype(BF16)
    )
    left = acc_ref[...].T
    done = jnp.zeros((128, cols), F32)
    for _ in range(3):
        piece = left.astype(BF16)
        done = done + lax.dot_general(
            piece, back, (((1,), (1,)), ((), ())), preferred_element_type=F32
        )
        left = left - piece.astype(F32)
    for ct in range(3):
        out_ref[0, pl.ds(ct, lanes, stride=3), :] = done[:lanes, ct * 128 : (ct + 1) * 128]


def beta_first_kernel(
    x_ref, tgt_ref, row_ref, w_ref, out_ref, table_ref, wt_ref, acc_ref, stage_ref
):
    @pl.when(pl.program_id(0) == 0)
    def _():
        build_table(x_ref, table_ref, stage_ref)

    beta_block(table_ref, tgt_ref, row_ref, w_ref, out_ref, wt_ref, acc_ref)


def beta_rest_kernel(table_ref, tgt_ref, row_ref, w_ref, old_ref, out_ref, wt_ref, acc_ref):
    beta_block(table_ref, tgt_ref, row_ref, w_ref, out_ref, wt_ref, acc_ref)


def list_specs(skip):
    return [
        pl.BlockSpec((8192,), lambda j: (j + skip,), memory_space=pltpu.SMEM),
        pl.BlockSpec((1, 64, 128), lambda j: (j + skip, 0, 0)),
        pl.BlockSpec((1, 48, 128), lambda j: (j + skip, 0, 0)),
    ]


def beta_params(blocks):
    return dict(
        compiler_params=pltpu.CompilerParams(vmem_limit_bytes=VMEM_LIMIT),
        cost_estimate=pl.CostEstimate(
            flops=blocks * 8 * 10**8, bytes_accessed=blocks * 2**20, transcendentals=0
        ),
    )


def beta_first(x2, numbers, weights, blocks):
    nbeta, rows, _ = x2.shape
    height = nbeta * 384 + 2 * PAD
    return pl.pallas_call(
        beta_first_kernel,
        out_shape=(
            jax.ShapeDtypeStruct((nbeta, rows, 128), F32),
            jax.ShapeDtypeStruct((height, 128), F32),
        ),
        grid=(blocks,),
        in_specs=[pl.BlockSpec((nbeta, rows, 128), lambda j: (0, 0, 0))] + list_specs(0),
        out_specs=(
            pl.BlockSpec((1, rows, 128), lambda j: (j, 0, 0)),
            pl.BlockSpec((height, 128), lambda j: (0, 0)),
        ),
        scratch_shapes=[
            pltpu.VMEM((384, 128), F32),
            pltpu.VMEM((384, 128), F32),
            pltpu.VMEM((rows, 128), F32),
        ],
        name="beta_first",
        **beta_params(blocks),
    )(x2, numbers.reshape(-1), numbers, weights)


def beta_rest(table, numbers, weights, partial, skip):
    nbeta, rows, _ = partial.shape
    return pl.pallas_call(
        beta_rest_kernel,
        out_shape=jax.ShapeDtypeStruct(partial.shape, F32),
        grid=(nbeta - skip,),
        in_specs=[pl.BlockSpec(table.shape, lambda j: (0, 0))]
        + list_specs(skip)
        + [pl.BlockSpec(memory_space=pl.ANY)],
        out_specs=pl.BlockSpec((1, rows, 128), lambda j: (j + skip, 0, 0)),
        scratch_shapes=[pltpu.VMEM((384, 128), F32), pltpu.VMEM((384, 128), F32)],
        input_output_aliases={4: 0},
        name="beta_rest",
        **beta_params(nbeta - skip),
    )(table, numbers.reshape(-1), numbers, weights, partial)


def alpha_kernel(
    own_ref,
    tbl_hbm,
    tgt_ref,
    w_ref,
    diag_ref,
    order_ref,
    out_ref,
    table_ref,
    wt_ref,
    acc_ref,
    buf_ref,
    sem,
):
    chunk = buf_ref.shape[1]
    total = tbl_hbm.shape[0]
    n = total // chunk
    exc = w_ref.shape[0]
    rows = diag_ref.shape[0]

    def fetch(k):
        return pltpu.make_async_copy(
            tbl_hbm.at[pl.ds(k * chunk, chunk), :], buf_ref.at[k], sem.at[k]
        )

    for k in range(n):
        fetch(k).start()
    for k in range(rows // 128):
        turned = jnp.concatenate(
            [w_ref[:, k * 128 : (k + 1) * 128], jnp.zeros((128 - exc, 128), F32)], axis=0
        ).T
        for ct in range(3):
            wt_ref[pl.ds(k * 384 + ct, 128, stride=3), :] = turned

    for k in range(n):
        fetch(k).wait()

        def widen(i, carry):
            start = pl.multiple_of(i * 128, 128)
            table_ref[pl.ds(pl.multiple_of(start + (k * chunk + PAD), 8), 128), :] = buf_ref[
                k, pl.ds(start, 128), :
            ].astype(F32)
            return carry

        lax.fori_loop(0, chunk // 128, widen, 0)
    sub = lax.broadcasted_iota(jnp.int32, (8, 128), 0)
    buckets = exc // STEPS
    ids = exc * rows
    at = ids + rows

    front = sub < 3
    back = jnp.logical_and(sub >= 3, sub < 6)

    def make(depth):
        def group(g, carry):
            first = pl.multiple_of(g * 8, 8)
            near = tgt_ref.at[pl.ds(first, ids + 8)]
            w6 = [wt_ref[pl.ds(first * 3 + 6 * q, 8), :] for q in range(4)]
            acc = [jnp.zeros((8, 128), F32)] * 4
            for e in range(depth):
                for q in range(4):
                    low = table_ref[pl.ds(near[e * rows + 2 * q] + PAD, 8), :]
                    high = table_ref[pl.ds(near[e * rows + 2 * q + 1] + (PAD - 3), 8), :]
                    w = jnp.broadcast_to(w6[q][:, e : e + 1], (8, 128))
                    acc[q] = acc[q] + jnp.where(front, low, high) * w
            for q in range(4):
                low = near[ids + 2 * q] + PAD
                high = near[ids + 2 * q + 1] + (PAD - 3)
                pltpu.store(acc_ref.at[pl.ds(low, 8), :], acc[q], mask=front)
                pltpu.store(acc_ref.at[pl.ds(high, 8), :], acc[q], mask=back)
            return carry

        return group

    for k in reversed(range(buckets)):
        begin = tgt_ref[at + k + 1] if k + 1 < buckets else 0
        lax.fori_loop(begin, tgt_ref[at + k], make((k + 1) * STEPS), 0)

    own = own_ref[0]

    def finish(i, carry):
        for u in range(4):
            place = pl.multiple_of(i * 32 + u * 8, 8)
            for ct in range(3):
                spot = place * 3 + (ct + PAD)
                out_ref[pl.ds(place * 3 + ct, 8, stride=3), :] = (
                    acc_ref[pl.ds(spot, 8, stride=3), :]
                    + diag_ref[pl.ds(place, 8), ct * 128 : (ct + 1) * 128]
                    * table_ref[pl.ds(own * 3 + spot, 8, stride=3), :]
                )
        return carry

    lax.fori_loop(0, rows // 32, finish, 0)


def alpha_term(own, table, numbers, weights, diag, order):
    rows = diag.shape[0]
    total = table.shape[0]
    chunk = total // 8
    return pl.pallas_call(
        alpha_kernel,
        out_shape=jax.ShapeDtypeStruct((rows * 3, 128), F32),
        in_specs=[
            pl.BlockSpec(memory_space=pltpu.SMEM),
            pl.BlockSpec(memory_space=pl.ANY),
            pl.BlockSpec(memory_space=pltpu.SMEM),
            pl.BlockSpec(memory_space=pltpu.VMEM),
            pl.BlockSpec(memory_space=pltpu.VMEM),
            pl.BlockSpec(memory_space=pl.ANY),
        ],
        out_specs=pl.BlockSpec(memory_space=pltpu.VMEM),
        scratch_shapes=[
            pltpu.VMEM((total + 4 * PAD, 128), F32),
            pltpu.VMEM((rows * 3 + PAD, 128), F32),
            pltpu.VMEM((rows * 3 + 4 * PAD, 128), F32),
            pltpu.VMEM((8, chunk, 128), BF16),
            pltpu.SemaphoreType.DMA((8,)),
        ],
        compiler_params=pltpu.CompilerParams(vmem_limit_bytes=VMEM_LIMIT),
        cost_estimate=pl.CostEstimate(
            flops=10**10, bytes_accessed=16 * 2**20, transcendentals=0
        ),
        name="alpha_term",
    )(own, table, numbers, weights, diag, order)


def merge_kernel(nalpha, alpha_ref, beta_ref, out_ref):
    nbeta = beta_ref.shape[0]
    pieces = out_ref.shape[1]

    def senders(beta_s, carry):
        for alpha_s in range(nalpha):
            p = alpha_s * nbeta + beta_s
            one = alpha_ref[pl.ds(p * pieces, pieces), :]
            other = beta_ref[beta_s, alpha_s * pieces : (alpha_s + 1) * pieces, :]
            out_ref[p] = (one + other).astype(BF16)
        return carry

    lax.fori_loop(0, nbeta, senders, 0)


def merge(alpha, beta, nalpha, pieces):
    devices = nalpha * beta.shape[0]
    return pl.pallas_call(
        functools.partial(merge_kernel, nalpha),
        out_shape=jax.ShapeDtypeStruct((devices, pieces, 128), BF16),
        compiler_params=pltpu.CompilerParams(vmem_limit_bytes=VMEM_LIMIT),
        name="merge",
    )(alpha, beta)


def finish_kernel(entries, parts_ref, sigma_ref, coef_ref, out_ref, rms_ref):
    parts = parts_ref[:, 0, :]
    square = parts[:, 0:1]
    total = jnp.sum(parts, axis=0, keepdims=True)
    rayleigh = total[:, 1:2] / total[:, 0:1]
    shift = rayleigh - parts[:, 3:4]
    rest = jnp.sum(parts[:, 2:3] + shift * shift * square, axis=0, keepdims=True)
    out_ref[...] = sigma_ref[...] - rayleigh * coef_ref[...]
    rms_ref[...] = jnp.sqrt(rest / entries)


def finish(parts, sigma, coef, entries):
    return pl.pallas_call(
        functools.partial(finish_kernel, float(entries)),
        out_shape=(
            jax.ShapeDtypeStruct(sigma.shape, F32),
            jax.ShapeDtypeStruct((1, 1), F32),
        ),
        name="finish",
    )(parts, sigma, coef)


def unpack_kernel(
    r_ref, key_ref, label_ref, coef_ref, tr_ref, sigma_ref, part_ref, stage_ref, half_ref
):
    devices, pieces, _ = r_ref.shape
    rows = devices * pieces // 2
    confs = key_ref.shape[1]
    width = coef_ref.shape[0]
    ncls = tr_ref.shape[0]
    tall = width + -width % 8

    def spread(p, carry):
        stage_ref[pl.ds(p * pieces, pieces), :] = r_ref[p].astype(F32)
        return carry

    lax.fori_loop(0, devices, spread, 0)
    for h in range(2):
        half_ref[:, h * 128 : (h + 1) * 128] = stage_ref[pl.ds(h, rows, stride=2), :].astype(BF16)
    key = key_ref[...]
    block = 256
    dets = jnp.zeros((256, confs), F32)
    for b in range(rows // block):
        onehot = (
            (lax.broadcasted_iota(jnp.int32, (block, confs), 0) + b * block == key)
            .astype(F32)
            .astype(BF16)
        )
        dets = dets + lax.dot_general(
            half_ref[pl.ds(b * block, block), :],
            onehot,
            (((0,), (0,)), ((), ())),
            preferred_element_type=F32,
        )
    trans = jnp.concatenate([padded(tr_ref, c) for c in range(ncls)], axis=0)
    products = jnp.dot(trans, dets, precision=HIGH, preferred_element_type=F32)
    sigma = jnp.zeros((width, confs), F32)
    for c in range(ncls):
        part = products[c * tall : c * tall + width]
        sigma = sigma + jnp.where(label_ref[0:1, :] == c, part, 0.0)
    coef = coef_ref[...]
    sigma_ref[...] = sigma
    square = jnp.sum(jnp.sum(coef * coef, axis=1, keepdims=True), axis=0, keepdims=True)
    cross = jnp.sum(jnp.sum(coef * sigma, axis=1, keepdims=True), axis=0, keepdims=True)
    ratio = jnp.where(square > 0.0, cross / jnp.where(square > 0.0, square, 1.0), 0.0)
    rest = sigma - ratio * coef
    rho = jnp.sum(jnp.sum(rest * rest, axis=1, keepdims=True), axis=0, keepdims=True)
    lane = lax.broadcasted_iota(jnp.int32, (1, 128), 1)
    part_ref[...] = jnp.where(
        lane == 0,
        square,
        jnp.where(lane == 1, cross, jnp.where(lane == 2, rho, jnp.where(lane == 3, ratio, 0.0))),
    )


def unpack(returned, key, labels, coef, transforms):
    return pl.pallas_call(
        unpack_kernel,
        out_shape=(
            jax.ShapeDtypeStruct(coef.shape, F32),
            jax.ShapeDtypeStruct((1, 128), F32),
        ),
        scratch_shapes=[
            pltpu.VMEM((returned.shape[0] * returned.shape[1], 128), F32),
            pltpu.VMEM((returned.shape[0] * returned.shape[1] // 2, 256), BF16),
        ],
        compiler_params=pltpu.CompilerParams(vmem_limit_bytes=VMEM_LIMIT),
        name="unpack",
    )(returned, key, labels, coef, transforms)


def exchange(x, axes):
    return lax.all_to_all(x, axes, split_axis=0, concat_axis=0, tiled=True)


def body(
    csf_coef,
    conf_class,
    conf_tile,
    transforms,
    alpha_targets,
    alpha_values,
    alpha_counts,
    beta_targets,
    beta_values,
    beta_counts,
    det_diag,
):
    nalpha = lax.axis_size("alpha")
    nbeta = lax.axis_size("beta")
    devices = nalpha * nbeta
    ncsf, confs = csf_coef.shape
    capacity = 3 * confs // devices
    rows_alpha = det_diag.shape[0]
    width = transforms.shape[2]
    exc = alpha_targets.shape[0]
    pieces = capacity * width // 128
    labels = jnp.stack([conf_class, conf_tile[:, 0]])
    bplan = plan(beta_targets, beta_values, beta_counts, STEPS)
    zero = jnp.zeros((1, bplan.shape[1]), F32)
    lists = jnp.concatenate(
        [
            bplan[:exc],
            bplan[3 * exc : 3 * exc + 1],
            zero,
            bplan[exc : 2 * exc],
            bplan[3 * exc + 1 : 3 * exc + 3],
            bplan[2 * exc : 3 * exc],
        ],
        axis=0,
    ).astype(BF16)
    lists = lists.reshape(-1, 128)
    lists = jnp.pad(lists, ((0, -lists.shape[0] % 16), (0, 0)))
    aplan = plan(alpha_targets, alpha_values, alpha_counts, STEPS)
    anumbers = jnp.concatenate(
        [
            aplan[:exc] * 384.0 + aplan[exc : 2 * exc] * 3.0,
            aplan[3 * exc : 3 * exc + 1] * 384.0 + aplan[3 * exc + 1 : 3 * exc + 2] * 3.0,
            aplan[3 * exc + 2 : 3 * exc + 3],
        ],
        axis=0,
    )
    anumbers = anumbers.astype(jnp.int32).reshape(-1)
    aweights = aplan[2 * exc : 3 * exc]

    body_rows = nalpha * pieces
    heard = exchange(jnp.broadcast_to(lists[None], (nbeta,) + lists.shape), "beta")
    labels, lists = lax.optimization_barrier((labels, lists))
    outgoing, key = pack(csf_coef, labels, transforms, capacity)
    outgoing, heard = lax.optimization_barrier((outgoing, heard))
    slab = exchange(outgoing.reshape(nalpha, nbeta * pieces, 128), "alpha")
    slab, anumbers, aweights = lax.optimization_barrier((slab, anumbers, aweights))
    x2 = (
        slab.reshape(nalpha, nbeta, pieces, 128)
        .transpose(1, 0, 2, 3)
        .reshape(nbeta, body_rows, 128)
    )
    nrows = (exc + 2) * (bplan.shape[1] // 128)
    wrows = exc * (bplan.shape[1] // 128)
    high = heard[:, :nrows].astype(jnp.int32)
    low = heard[:, nrows : 2 * nrows].astype(jnp.int32)
    bnumbers = jnp.pad(high * 128 + low, ((0, 0), (0, 64 - nrows), (0, 0)))
    bweights = heard[:, 2 * nrows : 2 * nrows + wrows].astype(F32)

    got = exchange(x2, "beta")
    beta_a, btable = beta_first(x2, bnumbers, bweights, FIRST)
    got, btable = lax.optimization_barrier((got, btable))
    flat = (
        got.reshape(nbeta, nalpha, pieces, 128).transpose(1, 0, 2, 3).reshape(-1, 128)
    )
    table = lax.all_gather(flat, "alpha", axis=0, tiled=True)
    beta_b = beta_rest(btable, bnumbers, bweights, beta_a, FIRST)
    beta_tile = exchange(beta_b, "beta")
    own = (lax.axis_index("alpha") * rows_alpha).astype(jnp.int32)[None]
    partial = alpha_term(own, table, anumbers, aweights, det_diag, beta_b)
    sigma_tile = merge(partial, beta_tile, nalpha, pieces)
    returned = exchange(sigma_tile, BOTH)
    sigma, part = unpack(returned, key, labels, csf_coef, transforms)
    parts = exchange(jnp.broadcast_to(part[None], (devices, 1, 128)), BOTH)
    residual, rms = finish(parts, sigma, csf_coef, ncsf * confs * devices)
    return (residual, rms[0, 0])


def solution(mesh):
    placed = (
        P(None, BOTH),
        P(BOTH),
        P(BOTH, None),
        P(),
        P(None, "alpha"),
        P(None, "alpha"),
        P("alpha"),
        P(None, "beta"),
        P(None, "beta"),
        P("beta"),
        P("alpha", "beta"),
    )
    return jax.shard_map(
        body,
        mesh=mesh,
        in_specs=placed,
        out_specs=(P(None, BOTH), P()),
        check_vma=False,
    )
```

profile of v0, /device:TPU:1, one launch (start us, length us, event | category | flops | bytes accessed | tf_op | source)
XLA Modules:
  0.0 272.6 jit_solution(4271898080659752518)
XLA Ops:
  7.2 0.0 copy-start.3
  7.2 0.0 copy-start.4
  7.2 1.2 broadcast_in_dim.27.cnt_ref
  8.4 1.9 plan.2
  10.4 0.9 convert.14
  11.3 0.4 concatenate.7
  11.8 0.9 broadcast_in_dim.29
  12.7 8.6 %all-to-all-start = ((bf16[16,160,128]{2,1,0:T(8,128)(2,1)}), bf16[16,160,128]{2,1,0:T(8,128)(2,1)S(1)}, u32[]{:S(2)}, u32[]{:S(2)}) async-start(bf16[16,160,128]{2,1,0:T(8,128)(2,1)} %broadcast_in_dim.29), calls=%async_computation | async-start | bytes 1310720 | tf_op jit(solution)/shard_map/all_to_all | solution.py:511
  21.3 0.0 copy-done.3
  21.3 0.0 copy-done.4
  21.3 0.6 pad_add_fusion.label_ref
  21.9 0.0 copy-done.2
  21.9 0.6 broadcast_in_dim.30.cnt_ref
  22.5 6.7 %pack.1 = (bf16[4608,128]{1,0:T(8,128)(2,1)}, s32[1,768]{1,0:T(1,128)}) custom-call(f32[42,768]{1,0:T(8,128)} %coef_ref.5, s32[2,768]{1,0:T(2,128)} %pad_add_fusion.label_ref, f32[6,42,256]{2,1,0:T(8,128)} %tr_ref.3), custom_call_target="tpu_custom_call" | custom-call | tf_op jit(solution)/shard_map/pack/pallas_call | solution.py:71
  29.2 4.4 %plan.3 = f32[56,1536]{1,0:T(8,128)} custom-call(s32[16,1536]{1,0:T(8,128)} %tgt_ref.3, bf16[16,1536]{1,0:T(8,128)(2,1)} %val_ref.3, s32[1,1536]{1,0:T(1,128)} %broadcast_in_dim.30.cnt_ref), custom_call_target="tpu_custom_call" | custom-call | tf_op jit(solution)/shard_map/plan/pallas_call | solution.py:138
  33.6 0.0 all-to-all-done
  33.6 5.9 %all-to-all-start.1 = ((bf16[8,576,128]{2,1,0:T(8,128)(2,1)}), bf16[8,576,128]{2,1,0:T(8,128)(2,1)S(1)}, u32[]{:S(2)}, u32[]{:S(2)}) async-start(bf16[8,576,128]{2,1,0:T(8,128)(2,1)} %bitcast.16), calls=%async_computation.1 | async-start | bytes 2359296 | tf_op jit(solution)/shard_map/all_to_all | solution.py:511
  39.5 0.0 copy-done.1
  39.5 0.6 fusion.2
  40.2 0.7 convert_element_type.25.tgt_ref
  40.8 15.0 %all-to-all-done.1 = bf16[8,576,128]{2,1,0:T(8,128)(2,1)S(1)} async-done(((bf16[8,576,128]{2,1,0:T(8,128)(2,1)}), bf16[8,576,128]{2,1,0:T(8,128)(2,1)S(1)}, u32[]{:S(2)}, u32[]{:S(2)}) %all-to-all-start.1) | async-done | bytes 1179680 | tf_op jit(solution)/shard_map/all_to_all | solution.py:511
  55.8 0.8 copy.19
  56.6 0.5 copy.20
  57.1 1.3 copy.21.x_ref
  58.4 6.4 %all-to-all-start.2 = ((bf16[16,288,128]{2,1,0:T(8,128)(2,1)}), bf16[16,288,128]{2,1,0:T(8,128)(2,1)S(1)}, u32[]{:S(2)}, u32[]{:S(2)}) async-start(bf16[16,288,128]{2,1,0:T(8,128)(2,1)} %copy.21.x_ref), calls=%async_computation.2 | async-start | bytes 2359296 | tf_op jit(solution)/shard_map/all_to_all | solution.py:511
  64.9 0.2 all-gather.2.cloned.1.call-start
  65.1 0.2 convert_add_fusion
  65.3 0.9 pad.9.row_ref
  66.2 0.8 slice_convert_fusion.w_ref
  67.0 27.2 %beta_first.1 = (f32[16,288,128]{2,1,0:T(8,128)}, f32[6160,128]{1,0:T(8,128)}) custom-call(bf16[16,288,128]{2,1,0:T(8,128)(2,1)} %copy.21.x_ref, s32[131072]{0:T(1024)} %bitcast.17, s32[16,64,128]{2,1,0:T(8,128)} %pad.9.row_ref, f32[16,48,128]{2,1,0:T(8,128)} %slice_convert_fusion.w_ref), custom_call_target="tpu_custom_call" | custom-call | flops 3200000000 | bytes 4194304 | tf_op jit(solution)/shard_map/beta_first/pallas_call | solution.py:229
  94.2 0.0 all-to-all-done.2
  94.2 0.5 copy.23
  94.6 0.3 copy.24
  95.0 1.2 reshape.38
  96.1 0.0 all-gather.2.cloned.1.call-update
  96.2 71.5 %beta_rest.1.order_ref = f32[16,288,128]{2,1,0:T(8,128)} custom-call(f32[6160,128]{1,0:T(8,128)} %get-tuple-element.27.table_ref, s32[131072]{0:T(1024)} %bitcast.18, s32[16,64,128]{2,1,0:T(8,128)} %pad.9.row_ref, f32[16,48,128]{2,1,0:T(8,128)} %slice_convert_fusion.w_ref, f32[16,288,128]{2,1,0:T(8,128)} %get-tuple-element.28.old_ref), custom_call_target="tpu_custom_call", output_to_operand_aliasing={{}: (4, {})} | custom-call | flops 9600000000 | bytes 12582912 | tf_op jit(solution)/shard_map/beta_rest/pallas_call | solution.py:253
  167.6 6.7 %all-to-all-start.3 = ((f32[16,288,128]{2,1,0:T(8,128)}), f32[16,288,128]{2,1,0:T(8,128)S(1)}, u32[]{:S(2)}, u32[]{:S(2)}) async-start(f32[16,288,128]{2,1,0:T(8,128)} %beta_rest.1.order_ref), calls=%async_computation.3 | async-start | bytes 4718592 | tf_op jit(solution)/shard_map/all_to_all | solution.py:511
  174.3 0.0 all-gather.2.cloned.1.call-done.tbl_hbm
  174.3 32.4 %alpha_term.1.alpha_ref = f32[4608,128]{1,0:T(8,128)} custom-call(s32[1]{0:T(128)} %bitcast.own_ref, bf16[36864,128]{1,0:T(8,128)(2,1)} %all-gather.2.cloned.1.call-done.tbl_hbm, s32[27648]{0:T(1024)} %convert_element_type.25.tgt_ref, f32[16,1536]{1,0:T(8,128)} %get-tuple-element.26.w_ref, f32[1536,384]{1,0:T(8,128)} %diag_ref.1, ...), custom_call_target="tpu_custom_call" | custom-call | flops 10000000000 | bytes 16777216 | tf_op jit(solution)/shard_map/alpha_term/pallas_call | solution.py:367
  206.7 0.0 all-to-all-done.3.beta_ref
  206.7 0.0 copy-start
  206.7 1.4 copy-done
  208.2 3.8 %merge.1 = bf16[128,36,128]{2,1,0:T(8,128)(2,1)} custom-call(f32[4608,128]{1,0:T(8,128)} %alpha_term.1.alpha_ref, f32[16,288,128]{2,1,0:T(8,128)} %copy-done), custom_call_target="tpu_custom_call" | custom-call | tf_op jit(solution)/shard_map/merge/pallas_call | solution.py:411
  212.0 30.6 %all_to_all.30.r_ref = bf16[128,36,128]{2,1,0:T(8,128)(2,1)} all-to-all(bf16[128,36,128]{2,1,0:T(8,128)(2,1)} %merge.1), channel_id=1, replica_groups=mesh['alpha'=8,'beta'=16] {'alpha','beta'}, dimensions={0} | all-to-all | bytes 2359296 | tf_op jit(solution)/shard_map/all_to_all | solution.py:511
  242.5 5.6 %unpack.1 = (f32[42,768]{1,0:T(8,128)}, f32[1,128]{1,0:T(1,128)}) custom-call(bf16[128,36,128]{2,1,0:T(8,128)(2,1)} %all_to_all.30.r_ref, s32[1,768]{1,0:T(1,128)} %get-tuple-element.29.key_ref, s32[2,768]{1,0:T(2,128)} %pad_add_fusion.label_ref, f32[42,768]{1,0:T(8,128)} %coef_ref.5, f32[6,42,256]{2,1,0:T(8,128)} %tr_ref.3), custom_call_target="tpu_custom_call" | custom-call | tf_op jit(solution)/shard_map/unpack/pallas_call | solution.py:495
  248.1 0.7 broadcast_in_dim.32
  248.8 15.1 %all_to_all.31.parts_ref = f32[128,1,128]{2,1,0:T(1,128)} all-to-all(f32[128,1,128]{2,1,0:T(1,128)S(1)} %broadcast_in_dim.32), channel_id=1, replica_groups=mesh['alpha'=8,'beta'=16] {'alpha','beta'}, dimensions={0} | all-to-all | bytes 131072 | tf_op jit(solution)/shard_map/all_to_all | solution.py:511
  263.9 1.9 finish.1
  (11 shorter events, 0.1 us)
Async XLA Ops:
  7.2 14.1 %copy-start.3 = (s32[768]{0:T(1024)S(1)}, s32[768]{0:T(1024)}, u32[]{:S(2)}) copy-start(s32[768]{0:T(1024)} %param.12) | copy-start | bytes 9220
  7.2 14.1 %copy-start.4 = (s32[768,1]{0,1:T(1,128)S(1)}, s32[768,1]{0,1:T(1,128)}, u32[]{:S(2)}) copy-start(s32[768,1]{0,1:T(1,128)} %param.13) | copy-start | bytes 9220
  8.4 13.5 %copy-start.2 = (s32[1536]{0:T(1024)S(1)}, s32[1536]{0:T(1024)}, u32[]{:S(2)}) copy-start(s32[1536]{0:T(1024)} %param.17) | copy-start | bytes 18436
  12.7 20.9 %all-to-all-start = ((bf16[16,160,128]{2,1,0:T(8,128)(2,1)}), bf16[16,160,128]{2,1,0:T(8,128)(2,1)S(1)}, u32[]{:S(2)}, u32[]{:S(2)}) async-start(bf16[16,160,128]{2,1,0:T(8,128)(2,1)} %broadcast_in_dim.29), calls=%async_computation | async-start | bytes 1310720 | tf_op jit(solution)/shard_map/all_to_all | solution.py:511
  33.6 5.9 %copy-start.1 = (f32[56,1536]{1,0:T(8,128)S(1)}, f32[56,1536]{1,0:T(8,128)}, u32[]{:S(2)}) copy-start(f32[56,1536]{1,0:T(8,128)} %plan.3) | copy-start | bytes 1032196
  33.6 22.2 %all-to-all-start.1 = ((bf16[8,576,128]{2,1,0:T(8,128)(2,1)}), bf16[8,576,128]{2,1,0:T(8,128)(2,1)S(1)}, u32[]{:S(2)}, u32[]{:S(2)}) async-start(bf16[8,576,128]{2,1,0:T(8,128)(2,1)} %bitcast.16), calls=%async_computation.1 | async-start | bytes 2359296 | tf_op jit(solution)/shard_map/all_to_all | solution.py:511
  58.4 35.7 %all-to-all-start.2 = ((bf16[16,288,128]{2,1,0:T(8,128)(2,1)}), bf16[16,288,128]{2,1,0:T(8,128)(2,1)S(1)}, u32[]{:S(2)}, u32[]{:S(2)}) async-start(bf16[16,288,128]{2,1,0:T(8,128)(2,1)} %copy.21.x_ref), calls=%async_computation.2 | async-start | bytes 2359296 | tf_op jit(solution)/shard_map/all_to_all | solution.py:511
  64.9 109.4 %all-gather.2.cloned.1.call-start = ((), (), s32[]{:S(2)}) async-start(), calls=%async_computation.6 | async-start | bytes 10616832 | tf_op jit(solution)/shard_map/all_gather | solution.py:589
  167.6 39.1 %all-to-all-start.3 = ((f32[16,288,128]{2,1,0:T(8,128)}), f32[16,288,128]{2,1,0:T(8,128)S(1)}, u32[]{:S(2)}, u32[]{:S(2)}) async-start(f32[16,288,128]{2,1,0:T(8,128)} %beta_rest.1.order_ref), calls=%async_computation.3 | async-start | bytes 4718592 | tf_op jit(solution)/shard_map/all_to_all | solution.py:511
  206.7 1.4 copy-start
Sparse Core Ops, SparseCore 0:
  96.3 54.7 all-gather.1
where the time goes:
time: 273 us
  Pallas kernels  155 us (57%)
  blocking collectives  45.6 us (17%)
  starting transfers between devices  27.8 us (10%)
  waiting for transfers between devices  15.1 us (6%)
  between operations  14.2 us (5%)
  local copies, waits for them, and re-layouts  11.4 us (4%)
  other arithmetic  3.16 us (1%)
    pallas_call x1, Pallas kernels, beta_rest(): pl.pallas_call(beta_rest_kernel, out_shape=jax.ShapeDtypeStruct(partial.s...  71.5 us
    all_to_all x2, blocking collectives, exchange(): return lax.all_to_all(x, axes, split_axis=0, concat_axis=0, tiled=True)  45.6 us
    pallas_call x1, Pallas kernels, alpha_term(): pl.pallas_call(alpha_kernel, out_shape=jax.ShapeDtypeStruct((rows * 3, 12...  32.4 us
    all_to_all x4, starting transfers between devices, exchange(): return lax.all_to_all(x, axes, split_axis=0, concat_axis=0, tiled=True)  27.6 us
    pallas_call x1, Pallas kernels, beta_first(): pl.pallas_call(beta_first_kernel, out_shape=(jax.ShapeDtypeStruct((nbeta,...  27.2 us
    all_to_all x4, waiting for transfers between devices, exchange(): return lax.all_to_all(x, axes, split_axis=0, concat_axis=0, tiled=True)  15 us
    pallas_call x1, Pallas kernels, pack(): pl.pallas_call(functools.partial(pack_kernel, capacity), out_shape=(jax.S...  6.67 us
    pallas_call x2, Pallas kernels, plan(): pl.pallas_call(functools.partial(plan_kernel, steps), out_shape=jax.Shape...  6.34 us
  transfers between devices with their start and end apart: 5, of which 1 were waited for; matrix products, arithmetic and copies ran while one was open for 2% of the time, Pallas kernels for 52%

commit v1 on v0

--- a/solution.py
+++ b/solution.py
@@ -13,8 +13,10 @@
 HIGH = lax.Precision.HIGHEST
 BOTH = ("alpha", "beta")
 PAD = 8
-FIRST = 4
+FIRST = 2
 STEPS = 2
+WIDE = 32
+FEW = 16
 VMEM_LIMIT = 60 * 1024 * 1024
 
 
@@ -80,23 +82,24 @@
     )(coef, labels, transforms)
 
 
-def build_table(x_ref, table_ref, stage_ref):
-    blocks, rows, _ = x_ref.shape
+def build_table(slab_refs, table_ref, stage_ref):
+    blocks, rows, _ = slab_refs[0].shape
     lanes = rows // 3
 
     def build(j, carry):
-        stage_ref[...] = x_ref[j].astype(F32)
-        for ct in range(3):
-            piece = stage_ref[pl.ds(ct, lanes, stride=3), :]
-            piece = jnp.concatenate([piece, jnp.zeros((128 - lanes, 128), F32)], axis=0)
-            start = pl.multiple_of((j * 3 + ct) * 128 + PAD, 8)
-            table_ref[pl.ds(start, 128), :] = piece.T
+        for h, slab_ref in enumerate(slab_refs):
+            stage_ref[...] = slab_ref[j].astype(F32)
+            for ct in range(3):
+                piece = stage_ref[pl.ds(ct, lanes, stride=3), :]
+                piece = jnp.concatenate([piece, jnp.zeros((128 - lanes, 128), F32)], axis=0)
+                start = (j * 3 + ct) * 256 + (PAD + h)
+                table_ref[pl.ds(start, 128, stride=2), :] = piece.T
         return carry
 
     lax.fori_loop(0, blocks, build, 0)
 
 
-def plan_kernel(steps, tgt_ref, val_ref, cnt_ref, out_ref):
+def plan_kernel(steps, width, tgt_ref, val_ref, cnt_ref, out_ref):
     exc, length = tgt_ref.shape
     counts = cnt_ref[...]
     place = lax.broadcasted_iota(jnp.int32, (1, length), 1)
@@ -127,83 +130,89 @@
     bounds = jnp.zeros((8, length), F32)
     for k in range(exc // steps):
         over = jnp.sum(jnp.where(counts > k * steps, 1.0, 0.0), axis=1, keepdims=True)
-        groups = ((over.astype(jnp.int32) + 7) >> 3).astype(F32)
+        groups = ((over.astype(jnp.int32) + (width - 1)) // width).astype(F32)
         bounds = jnp.where(jnp.logical_and(lane == k, rows == 2), groups, bounds)
     out_ref[0 : 3 * exc, :] = total[: 3 * exc]
     out_ref[3 * exc :, :] = jnp.where(rows == 2, bounds, total[3 * exc :])
 
 
-def plan(targets, values, counts, steps):
+def plan(targets, values, counts, steps, width):
     exc, length = targets.shape
     return pl.pallas_call(
-        functools.partial(plan_kernel, steps),
+        functools.partial(plan_kernel, steps, width),
         out_shape=jax.ShapeDtypeStruct((3 * exc + 8, length), F32),
         compiler_params=pltpu.CompilerParams(vmem_limit_bytes=VMEM_LIMIT),
         name="plan",
     )(targets, values, counts[None, :])
 
 
-def beta_block(table_ref, tgt_ref, row_ref, w_ref, out_ref, wt_ref, acc_ref):
-    lanes = out_ref.shape[1] // 3
+def beta_block(table_ref, tgt_ref, row_ref, w_ref, out_refs, wt_ref, acc_ref):
+    lanes = out_refs[0].shape[1] // 3
     exc = 16
     cols = 384
-    sub = lax.broadcasted_iota(jnp.int32, (8, 128), 0)
+    slot = lax.broadcasted_iota(jnp.int32, (8, 128), 0) >> 1
     for ct in range(3):
-        wt_ref[pl.ds(ct * 128, 128), :] = jnp.concatenate(
+        turned = jnp.concatenate(
             [w_ref[0, pl.ds(ct, exc, stride=3), :], jnp.zeros((128 - exc, 128), F32)], axis=0
         ).T
+        for h in range(2):
+            wt_ref[pl.ds(ct * 256 + h, 128, stride=2), :] = turned
     buckets = exc // STEPS
     at = (exc + 1) * cols
 
     def make(depth):
         def group(g, carry):
-            first = pl.multiple_of(g * 8, 8)
-            near = tgt_ref.at[pl.ds(first, exc * cols)]
-            w8 = wt_ref[pl.ds(first, 8), :]
-            acc = jnp.zeros((8, 128), F32)
-            for e in range(depth):
-                got = None
-                for s in range(8):
-                    t = near[e * cols + s]
-                    win = table_ref[pl.ds(t + (PAD - s), 8), :]
-                    got = win if s == 0 else jnp.where(sub == s, win, got)
-                acc = acc + got * w8[:, e : e + 1]
-            acc_ref[pl.ds(first, 8), :] = acc
+            near = tgt_ref.at[pl.ds(g * FEW, exc * cols)]
+            for v in range(FEW // 4):
+                first = pl.multiple_of(g * (2 * FEW) + v * 8, 8)
+                w8 = wt_ref[pl.ds(first, 8), :]
+                acc = jnp.zeros((8, 128), F32)
+                for e in range(depth):
+                    got = None
+                    for s in range(4):
+                        t = near[e * cols + 4 * v + s]
+                        win = table_ref[pl.ds(t + (PAD - 2 * s), 8), :]
+                        got = win if s == 0 else jnp.where(slot == s, win, got)
+                    acc = acc + got * w8[:, e : e + 1]
+                acc_ref[pl.ds(first, 8), :] = acc
             return carry
 
         return group
 
     for k in reversed(range(buckets)):
-        begin = tgt_ref[at + k + 1] if k + 1 < buckets else 0
-        lax.fori_loop(begin, tgt_ref[at + k], make((k + 1) * STEPS), 0)
+        begin = tgt_ref[at + k + 1] >> 1 if k + 1 < buckets else 0
+        lax.fori_loop(begin, tgt_ref[at + k] >> 1, make((k + 1) * STEPS), 0)
     ids = jnp.concatenate([row_ref[0, exc * 3 + ct : exc * 3 + ct + 1, :] for ct in range(3)], axis=1)
     back = (
-        (lax.broadcasted_iota(jnp.int32, (cols, cols), 0) == ids).astype(F32).astype(BF16)
-    )
-    left = acc_ref[...].T
-    done = jnp.zeros((128, cols), F32)
-    for _ in range(3):
-        piece = left.astype(BF16)
-        done = done + lax.dot_general(
-            piece, back, (((1,), (1,)), ((), ())), preferred_element_type=F32
-        )
-        left = left - piece.astype(F32)
-    for ct in range(3):
-        out_ref[0, pl.ds(ct, lanes, stride=3), :] = done[:lanes, ct * 128 : (ct + 1) * 128]
+        (lax.broadcasted_iota(jnp.int32, (cols, cols), 0) * 2 == ids).astype(F32).astype(BF16)
+    )
+    for h, out_ref in enumerate(out_refs):
+        left = acc_ref[pl.ds(h, cols, stride=2), :].T
+        done = jnp.zeros((128, cols), F32)
+        for _ in range(3):
+            piece = left.astype(BF16)
+            done = done + lax.dot_general(
+                piece, back, (((1,), (1,)), ((), ())), preferred_element_type=F32
+            )
+            left = left - piece.astype(F32)
+        for ct in range(3):
+            out_ref[0, pl.ds(ct, lanes, stride=3), :] = done[:lanes, ct * 128 : (ct + 1) * 128]
 
 
 def beta_first_kernel(
-    x_ref, tgt_ref, row_ref, w_ref, out_ref, table_ref, wt_ref, acc_ref, stage_ref
+    x_ref, y_ref, tgt_ref, row_ref, w_ref, own_ref, far_ref, table_ref, wt_ref, acc_ref, stage_ref
 ):
     @pl.when(pl.program_id(0) == 0)
     def _():
-        build_table(x_ref, table_ref, stage_ref)
-
-    beta_block(table_ref, tgt_ref, row_ref, w_ref, out_ref, wt_ref, acc_ref)
-
-
-def beta_rest_kernel(table_ref, tgt_ref, row_ref, w_ref, old_ref, out_ref, wt_ref, acc_ref):
-    beta_block(table_ref, tgt_ref, row_ref, w_ref, out_ref, wt_ref, acc_ref)
+        build_table((x_ref, y_ref), table_ref, stage_ref)
+
+    beta_block(table_ref, tgt_ref, row_ref, w_ref, (own_ref, far_ref), wt_ref, acc_ref)
+
+
+def beta_rest_kernel(
+    table_ref, tgt_ref, row_ref, w_ref, old_own, old_far, own_ref, far_ref, wt_ref, acc_ref
+):
+    beta_block(table_ref, tgt_ref, row_ref, w_ref, (own_ref, far_ref), wt_ref, acc_ref)
 
 
 def list_specs(skip):
@@ -223,46 +232,51 @@
     )
 
 
-def beta_first(x2, numbers, weights, blocks):
+def beta_first(x2, y2, numbers, weights, blocks):
     nbeta, rows, _ = x2.shape
-    height = nbeta * 384 + 2 * PAD
+    half = numbers.shape[0]
+    height = 2 * nbeta * 384 + 2 * PAD
+    piece = pl.BlockSpec((1, rows, 128), lambda j: (j, 0, 0))
+    slab = pl.BlockSpec((nbeta, rows, 128), lambda j: (0, 0, 0))
     return pl.pallas_call(
         beta_first_kernel,
         out_shape=(
-            jax.ShapeDtypeStruct((nbeta, rows, 128), F32),
+            jax.ShapeDtypeStruct((half, rows, 128), F32),
+            jax.ShapeDtypeStruct((half, rows, 128), F32),
             jax.ShapeDtypeStruct((height, 128), F32),
         ),
         grid=(blocks,),
-        in_specs=[pl.BlockSpec((nbeta, rows, 128), lambda j: (0, 0, 0))] + list_specs(0),
-        out_specs=(
-            pl.BlockSpec((1, rows, 128), lambda j: (j, 0, 0)),
-            pl.BlockSpec((height, 128), lambda j: (0, 0)),
-        ),
+        in_specs=[slab, slab] + list_specs(0),
+        out_specs=(piece, piece, pl.BlockSpec((height, 128), lambda j: (0, 0))),
         scratch_shapes=[
-            pltpu.VMEM((384, 128), F32),
-            pltpu.VMEM((384, 128), F32),
+            pltpu.VMEM((768, 128), F32),
+            pltpu.VMEM((768, 128), F32),
             pltpu.VMEM((rows, 128), F32),
         ],
         name="beta_first",
         **beta_params(blocks),
-    )(x2, numbers.reshape(-1), numbers, weights)
-
-
-def beta_rest(table, numbers, weights, partial, skip):
-    nbeta, rows, _ = partial.shape
+    )(x2, y2, numbers.reshape(-1), numbers, weights)
+
+
+def beta_rest(table, numbers, weights, own, far, skip):
+    half, rows, _ = own.shape
+    piece = pl.BlockSpec((1, rows, 128), lambda j: (j + skip, 0, 0))
     return pl.pallas_call(
         beta_rest_kernel,
-        out_shape=jax.ShapeDtypeStruct(partial.shape, F32),
-        grid=(nbeta - skip,),
+        out_shape=(
+            jax.ShapeDtypeStruct(own.shape, F32),
+            jax.ShapeDtypeStruct(own.shape, F32),
+        ),
+        grid=(half - skip,),
         in_specs=[pl.BlockSpec(table.shape, lambda j: (0, 0))]
         + list_specs(skip)
-        + [pl.BlockSpec(memory_space=pl.ANY)],
-        out_specs=pl.BlockSpec((1, rows, 128), lambda j: (j + skip, 0, 0)),
-        scratch_shapes=[pltpu.VMEM((384, 128), F32), pltpu.VMEM((384, 128), F32)],
-        input_output_aliases={4: 0},
+        + [pl.BlockSpec(memory_space=pl.ANY)] * 2,
+        out_specs=(piece, piece),
+        scratch_shapes=[pltpu.VMEM((768, 128), F32), pltpu.VMEM((768, 128), F32)],
+        input_output_aliases={4: 0, 5: 1},
         name="beta_rest",
-        **beta_params(nbeta - skip),
-    )(table, numbers.reshape(-1), numbers, weights, partial)
+        **beta_params(half - skip),
+    )(table, numbers.reshape(-1), numbers, weights, own, far)
 
 
 def alpha_kernel(
@@ -320,17 +334,17 @@
 
     def make(depth):
         def group(g, carry):
-            first = pl.multiple_of(g * 8, 8)
-            near = tgt_ref.at[pl.ds(first, ids + 8)]
-            w6 = [wt_ref[pl.ds(first * 3 + 6 * q, 8), :] for q in range(4)]
-            acc = [jnp.zeros((8, 128), F32)] * 4
+            first = pl.multiple_of(g * WIDE, WIDE)
+            near = tgt_ref.at[pl.ds(first, ids + WIDE)]
+            w6 = [wt_ref[pl.ds(first * 3 + 6 * q, 8), :] for q in range(WIDE // 2)]
+            acc = [jnp.zeros((8, 128), F32)] * (WIDE // 2)
             for e in range(depth):
-                for q in range(4):
+                for q in range(WIDE // 2):
                     low = table_ref[pl.ds(near[e * rows + 2 * q] + PAD, 8), :]
                     high = table_ref[pl.ds(near[e * rows + 2 * q + 1] + (PAD - 3), 8), :]
                     w = jnp.broadcast_to(w6[q][:, e : e + 1], (8, 128))
                     acc[q] = acc[q] + jnp.where(front, low, high) * w
-            for q in range(4):
+            for q in range(WIDE // 2):
                 low = near[ids + 2 * q] + PAD
                 high = near[ids + 2 * q + 1] + (PAD - 3)
                 pltpu.store(acc_ref.at[pl.ds(low, 8), :], acc[q], mask=front)
@@ -534,7 +548,7 @@
     exc = alpha_targets.shape[0]
     pieces = capacity * width // 128
     labels = jnp.stack([conf_class, conf_tile[:, 0]])
-    bplan = plan(beta_targets, beta_values, beta_counts, STEPS)
+    bplan = plan(beta_targets, beta_values, beta_counts, STEPS, FEW)
     zero = jnp.zeros((1, bplan.shape[1]), F32)
     lists = jnp.concatenate(
         [
@@ -549,7 +563,7 @@
     ).astype(BF16)
     lists = lists.reshape(-1, 128)
     lists = jnp.pad(lists, ((0, -lists.shape[0] % 16), (0, 0)))
-    aplan = plan(alpha_targets, alpha_values, alpha_counts, STEPS)
+    aplan = plan(alpha_targets, alpha_values, alpha_counts, STEPS, WIDE)
     anumbers = jnp.concatenate(
         [
             aplan[:exc] * 384.0 + aplan[exc : 2 * exc] * 3.0,
@@ -575,22 +589,33 @@
     )
     nrows = (exc + 2) * (bplan.shape[1] // 128)
     wrows = exc * (bplan.shape[1] // 128)
-    high = heard[:, :nrows].astype(jnp.int32)
-    low = heard[:, nrows : 2 * nrows].astype(jnp.int32)
-    bnumbers = jnp.pad(high * 128 + low, ((0, 0), (0, 64 - nrows), (0, 0)))
-    bweights = heard[:, 2 * nrows : 2 * nrows + wrows].astype(F32)
+    half = nbeta // 2
+    side = lax.axis_index("alpha") % 2
+    swap = [(i, i ^ 1) for i in range(nalpha)]
+    y2 = lax.ppermute(x2, "alpha", swap)
+    mine = lax.dynamic_slice_in_dim(heard, side * half, half, axis=0)
+    high = mine[:, :nrows].astype(jnp.int32)
+    low = mine[:, nrows : 2 * nrows].astype(jnp.int32)
+    bnumbers = jnp.pad(high * 256 + low * 2, ((0, 0), (0, 64 - nrows), (0, 0)))
+    bweights = mine[:, 2 * nrows : 2 * nrows + wrows].astype(F32)
 
     got = exchange(x2, "beta")
-    beta_a, btable = beta_first(x2, bnumbers, bweights, FIRST)
+    near_a, far_a, btable = beta_first(x2, y2, bnumbers, bweights, FIRST)
     got, btable = lax.optimization_barrier((got, btable))
     flat = (
         got.reshape(nbeta, nalpha, pieces, 128).transpose(1, 0, 2, 3).reshape(-1, 128)
     )
     table = lax.all_gather(flat, "alpha", axis=0, tiled=True)
-    beta_b = beta_rest(btable, bnumbers, bweights, beta_a, FIRST)
-    beta_tile = exchange(beta_b, "beta")
+    near_b, far_b = beta_rest(btable, bnumbers, bweights, near_a, far_a, FIRST)
+    back = lax.ppermute(far_b, "alpha", swap)
+    beta_slab = jnp.where(
+        side == 0,
+        jnp.concatenate([near_b, back], axis=0),
+        jnp.concatenate([back, near_b], axis=0),
+    )
+    beta_tile = exchange(beta_slab, "beta")
     own = (lax.axis_index("alpha") * rows_alpha).astype(jnp.int32)[None]
-    partial = alpha_term(own, table, anumbers, aweights, det_diag, beta_b)
+    partial = alpha_term(own, table, anumbers, aweights, det_diag, beta_slab)
     sigma_tile = merge(partial, beta_tile, nalpha, pieces)
     returned = exchange(sigma_tile, BOTH)
     sigma, part = unpack(returned, key, labels, csf_coef, transforms)

time: 273 us -> 237 us (0.87)
  Pallas kernels: 155 us -> 106 us
  waiting for transfers between devices: 15.1 us -> 26.1 us
  blocking collectives: 45.6 us -> 42.1 us
  other arithmetic: 3.16 us -> 6.23 us
    pallas_call x4, Pallas kernels: 105 us -> 59.1 us  [the longest x1 35.8 us: beta_rest(): pl.pallas_call(beta_rest_kernel, out_shape=(jax.ShapeDtypeStruct(own.shap...]
    all_gather x1, waiting for transfers between devices: 0.02 us -> 4.43 us  [body(): table = lax.all_gather(flat, 'alpha', axis=0, tiled=True)]
    pallas_call x1, Pallas kernels: 32.4 us -> 28.5 us  [alpha_term(): pl.pallas_call(alpha_kernel, out_shape=jax.ShapeDtypeStruct((rows * 3, 12...]
    all_to_all x4, waiting for transfers between devices: 15 us -> 18.7 us  [exchange(): return lax.all_to_all(x, axes, split_axis=0, concat_axis=0, tiled=True)]
    all_to_all x2, blocking collectives: 45.6 us -> 42.1 us  [exchange(): return lax.all_to_all(x, axes, split_axis=0, concat_axis=0, tiled=True)]
    select_n x0 -> x1, other arithmetic: none -> 3.25 us  [body(): jnp.where(side == 0, jnp.concatenate([near_b, back], axis=0), jnp.concate...]
    ppermute x0 -> x2, waiting for transfers between devices: none -> 2.93 us  [the longest x1 2.93 us: body(): back = lax.ppermute(far_b, 'alpha', swap)]
  transfers between devices with their start and end apart: 5 -> 7, of which waited for: 1 -> 4; matrix products, arithmetic and copies ran while one was open for 2% -> 3% of each run, Pallas kernels for 52% -> 39%
where the time goes in v1:
time: 237 us; the launch traced here: 236 us
  Pallas kernels  106 us (45%)
  blocking collectives  42.1 us (18%)
  starting transfers between devices  29.5 us (12%)
  waiting for transfers between devices  26.1 us (11%)
  between operations  14.2 us (6%)
  local copies, waits for them, and re-layouts  12.3 us (5%)
  other arithmetic  6.23 us (3%)
    all_to_all x2, blocking collectives, exchange(): return lax.all_to_all(x, axes, split_axis=0, concat_axis=0, tiled=True)  42.1 us
    pallas_call x1, Pallas kernels, beta_rest(): pl.pallas_call(beta_rest_kernel, out_shape=(jax.ShapeDtypeStruct(own.shap...  35.8 us
    pallas_call x1, Pallas kernels, alpha_term(): pl.pallas_call(alpha_kernel, out_shape=jax.ShapeDtypeStruct((rows * 3, 12...  28.5 us
    all_to_all x4, starting transfers between devices, exchange(): return lax.all_to_all(x, axes, split_axis=0, concat_axis=0, tiled=True)  27 us
    all_to_all x4, waiting for transfers between devices, exchange(): return lax.all_to_all(x, axes, split_axis=0, concat_axis=0, tiled=True)  18.7 us
    pallas_call x1, Pallas kernels, beta_first(): pl.pallas_call(beta_first_kernel, out_shape=(jax.ShapeDtypeStruct((half,...  16.9 us
    pallas_call x1, Pallas kernels, pack(): pl.pallas_call(functools.partial(pack_kernel, capacity), out_shape=(jax.S...  6.69 us
    pallas_call x2, Pallas kernels, plan(): pl.pallas_call(functools.partial(plan_kernel, steps, width), out_shape=ja...  6.35 us
  transfers between devices with their start and end apart: 7, of which 4 were waited for; matrix products, arithmetic and copies ran while one was open for 3% of the time, Pallas kernels for 39%

profile of v1, /device:TPU:1, one launch (start us, length us, event | category | flops | bytes accessed | tf_op | source)
XLA Modules:
  0.0 236.0 jit_solution(2267436622789361330)
XLA Ops:
  7.2 1.3 broadcast_in_dim.27.cnt_ref
  8.5 1.9 plan.2
  10.4 0.9 convert.14
  11.3 0.4 concatenate.13
  11.8 0.9 broadcast_in_dim.29
  12.7 8.6 %all-to-all-start = ((bf16[16,160,128]{2,1,0:T(8,128)(2,1)}), bf16[16,160,128]{2,1,0:T(8,128)(2,1)S(1)}, u32[]{:S(2)}, u32[]{:S(2)}) async-start(bf16[16,160,128]{2,1,0:T(8,128)(2,1)} %broadcast_in_dim.29), calls=%async_computation | async-start | bytes 1310720 | tf_op jit(solution)/shard_map/all_to_all | solution.py:525
  21.3 0.0 copy-done.4
  21.3 0.6 pad_add_fusion.label_ref
  22.0 0.6 broadcast_in_dim.30.cnt_ref
  22.5 6.7 %pack.1 = (bf16[4608,128]{1,0:T(8,128)(2,1)}, s32[1,768]{1,0:T(1,128)}) custom-call(f32[42,768]{1,0:T(8,128)} %coef_ref.5, s32[2,768]{1,0:T(2,128)} %pad_add_fusion.label_ref, f32[6,42,256]{2,1,0:T(8,128)} %tr_ref.3), custom_call_target="tpu_custom_call" | custom-call | tf_op jit(solution)/shard_map/pack/pallas_call | solution.py:73
  29.2 4.4 %plan.3 = f32[56,1536]{1,0:T(8,128)} custom-call(s32[16,1536]{1,0:T(8,128)} %tgt_ref.3, bf16[16,1536]{1,0:T(8,128)(2,1)} %val_ref.3, s32[1,1536]{1,0:T(1,128)} %broadcast_in_dim.30.cnt_ref), custom_call_target="tpu_custom_call" | custom-call | tf_op jit(solution)/shard_map/plan/pallas_call | solution.py:141
  33.7 0.0 all-to-all-done
  33.7 5.8 %all-to-all-start.1 = ((bf16[8,576,128]{2,1,0:T(8,128)(2,1)}), bf16[8,576,128]{2,1,0:T(8,128)(2,1)S(1)}, u32[]{:S(2)}, u32[]{:S(2)}) async-start(bf16[8,576,128]{2,1,0:T(8,128)(2,1)} %bitcast.16), calls=%async_computation.1 | async-start | bytes 2359296 | tf_op jit(solution)/shard_map/all_to_all | solution.py:525
  39.5 0.6 fusion.2
  40.2 0.7 convert_element_type.25.tgt_ref
  40.9 15.0 %all-to-all-done.1 = bf16[8,576,128]{2,1,0:T(8,128)(2,1)S(1)} async-done(((bf16[8,576,128]{2,1,0:T(8,128)(2,1)}), bf16[8,576,128]{2,1,0:T(8,128)(2,1)S(1)}, u32[]{:S(2)}, u32[]{:S(2)}) %all-to-all-start.1) | async-done | bytes 1179680 | tf_op jit(solution)/shard_map/all_to_all | solution.py:525
  55.9 0.8 copy.21
  56.6 0.5 copy.22
  57.1 1.3 copy.23.x_ref
  58.4 1.0 collective-permute-start
  59.4 6.5 %all-to-all-start.2 = ((bf16[16,288,128]{2,1,0:T(8,128)(2,1)}), bf16[16,288,128]{2,1,0:T(8,128)(2,1)S(1)}, u32[]{:S(2)}, u32[]{:S(2)}) async-start(bf16[16,288,128]{2,1,0:T(8,128)(2,1)} %copy.23.x_ref), calls=%async_computation.2 | async-start | bytes 2359296 | tf_op jit(solution)/shard_map/all_to_all | solution.py:525
  65.9 0.2 all-gather.2.cloned.1.call-start
  66.1 0.1 multiply_add_fusion
  66.2 0.7 pad.9.row_ref
  67.0 0.7 dynamic-slice_convert_fusion.w_ref
  67.7 0.0 collective-permute-done.y_ref
  67.7 1.1 copy-done.5
  68.7 16.9 %beta_first.1 = (f32[8,288,128]{2,1,0:T(8,128)}, f32[8,288,128]{2,1,0:T(8,128)}, f32[12304,128]{1,0:T(8,128)}) custom-call(bf16[16,288,128]{2,1,0:T(8,128)(2,1)} %copy.23.x_ref, bf16[16,288,128]{2,1,0:T(8,128)(2,1)} %copy-done.5, s32[65536]{0:T(1024)} %bitcast.17, s32[8,64,128]{2,1,0:T(8,128)} %pad.9.row_ref, f32[8,48,128]{2,1,0:T(8,128)} %dynamic-slice_convert_fusion.w_ref), custom_call_target="tpu_custom_call" | custom-call | flops 1600000000 | bytes 2097152 | tf_op jit(solution)/shard_map/beta_first/pallas_call | solution.py:241
  85.6 0.0 all-to-all-done.2
  85.6 0.5 copy.26
  86.1 0.3 copy.27
  86.4 1.1 reshape.38
  87.6 0.0 all-gather.2.cloned.1.call-update
  87.6 35.8 %beta_rest.1 = (f32[8,288,128]{2,1,0:T(8,128)}, f32[8,288,128]{2,1,0:T(8,128)}) custom-call(f32[12304,128]{1,0:T(8,128)} %get-tuple-element.30.table_ref, s32[65536]{0:T(1024)} %bitcast.18, s32[8,64,128]{2,1,0:T(8,128)} %pad.9.row_ref, f32[8,48,128]{2,1,0:T(8,128)} %dynamic-slice_convert_fusion.w_ref, ...), custom_call_target="tpu_custom_call", output_to_operand_aliasing={{0}: (4, {}), {1}: (5, {})} | custom-call | flops 4800000000 | bytes 6291456 | tf_op jit(solution)/shard_map/beta_rest/pallas_call | solution.py:264
  123.5 1.3 collective-permute-start.1
  124.7 2.9 %collective-permute-done.1 = f32[8,288,128]{2,1,0:T(8,128)S(1)} collective-permute-done((f32[8,288,128]{2,1,0:T(8,128)}, f32[8,288,128]{2,1,0:T(8,128)S(1)}, u32[]{:S(2)}, u32[]{:S(2)}) %collective-permute-start.1) | collective-permute-done | bytes 1179680 | tf_op jit(solution)/shard_map/ppermute | solution.py:610
  127.7 3.2 %maximum_select_fusion.order_ref = f32[16,288,128]{2,1,0:T(8,128)} fusion(f32[8,288,128]{2,1,0:T(8,128)S(1)} %collective-permute-done.1, f32[8,288,128]{2,1,0:T(8,128)} %get-tuple-element.33, pred[]{:T(512)S(6)} %eq.5), kind=kLoop, calls=%fused_computation | loop fusion | flops 1769472 | bytes 4718593 | tf_op jit(solution)/shard_map/jit(_where)/select_n | solution.py:611
  130.9 6.1 %all-to-all-start.3 = ((f32[16,288,128]{2,1,0:T(8,128)}), f32[16,288,128]{2,1,0:T(8,128)S(1)}, u32[]{:S(2)}, u32[]{:S(2)}) async-start(f32[16,288,128]{2,1,0:T(8,128)} %maximum_select_fusion.order_ref), calls=%async_computation.3 | async-start | bytes 4718592 | tf_op jit(solution)/shard_map/all_to_all | solution.py:525
  137.0 4.4 %all-gather.2.cloned.1.call-done.tbl_hbm = bf16[36864,128]{1,0:T(8,128)(2,1)} async-done(((bf16[4608,128]{1,0:T(8,128)(2,1)}), bf16[36864,128]{1,0:T(8,128)(2,1)}) %all-gather.2.cloned.1.call-update) | async-done | bytes 9437200 | tf_op jit(solution)/shard_map/all_gather | solution.py:608
  141.5 28.5 %alpha_term.1.alpha_ref = f32[4608,128]{1,0:T(8,128)} custom-call(s32[1]{0:T(128)} %bitcast.own_ref, bf16[36864,128]{1,0:T(8,128)(2,1)} %all-gather.2.cloned.1.call-done.tbl_hbm, s32[27648]{0:T(1024)} %convert_element_type.25.tgt_ref, f32[16,1536]{1,0:T(8,128)} %get-tuple-element.29.w_ref, f32[1536,384]{1,0:T(8,128)} %diag_ref.1, ...), custom_call_target="tpu_custom_call" | custom-call | flops 10000000000 | bytes 16777216 | tf_op jit(solution)/shard_map/alpha_term/pallas_call | solution.py:381
  170.0 3.7 %all-to-all-done.3.beta_ref = f32[16,288,128]{2,1,0:T(8,128)S(1)} async-done(((f32[16,288,128]{2,1,0:T(8,128)}), f32[16,288,128]{2,1,0:T(8,128)S(1)}, u32[]{:S(2)}, u32[]{:S(2)}) %all-to-all-start.3) | async-done | bytes 2359328 | tf_op jit(solution)/shard_map/all_to_all | solution.py:525
  173.7 1.4 copy-done
  175.1 3.8 %merge.1 = bf16[128,36,128]{2,1,0:T(8,128)(2,1)} custom-call(f32[4608,128]{1,0:T(8,128)} %alpha_term.1.alpha_ref, f32[16,288,128]{2,1,0:T(8,128)} %copy-done), custom_call_target="tpu_custom_call" | custom-call | tf_op jit(solution)/shard_map/merge/pallas_call | solution.py:425
  178.9 27.2 %all_to_all.30.r_ref = bf16[128,36,128]{2,1,0:T(8,128)(2,1)} all-to-all(bf16[128,36,128]{2,1,0:T(8,128)(2,1)} %merge.1), channel_id=1, replica_groups=mesh['alpha'=8,'beta'=16] {'alpha','beta'}, dimensions={0} | all-to-all | bytes 2359296 | tf_op jit(solution)/shard_map/all_to_all | solution.py:525
  206.1 5.6 %unpack.1 = (f32[42,768]{1,0:T(8,128)}, f32[1,128]{1,0:T(1,128)}) custom-call(bf16[128,36,128]{2,1,0:T(8,128)(2,1)} %all_to_all.30.r_ref, s32[1,768]{1,0:T(1,128)} %get-tuple-element.35.key_ref, s32[2,768]{1,0:T(2,128)} %pad_add_fusion.label_ref, f32[42,768]{1,0:T(8,128)} %coef_ref.5, f32[6,42,256]{2,1,0:T(8,128)} %tr_ref.3), custom_call_target="tpu_custom_call" | custom-call | tf_op jit(solution)/shard_map/unpack/pallas_call | solution.py:509
  211.7 0.7 broadcast_in_dim.32
  212.3 14.9 %all_to_all.31.parts_ref = f32[128,1,128]{2,1,0:T(1,128)} all-to-all(f32[128,1,128]{2,1,0:T(1,128)S(1)} %broadcast_in_dim.32), channel_id=1, replica_groups=mesh['alpha'=8,'beta'=16] {'alpha','beta'}, dimensions={0} | all-to-all | bytes 131072 | tf_op jit(solution)/shard_map/all_to_all | solution.py:525
  227.3 1.9 finish.1
  (18 shorter events, 0.1 us)
Async XLA Ops:
  7.2 14.2 %copy-start.3 = (s32[768]{0:T(1024)S(1)}, s32[768]{0:T(1024)}, u32[]{:S(2)}) copy-start(s32[768]{0:T(1024)} %param.12) | copy-start | bytes 9220
  7.2 14.2 %copy-start.4 = (s32[768,1]{0,1:T(1,128)S(1)}, s32[768,1]{0,1:T(1,128)}, u32[]{:S(2)}) copy-start(s32[768,1]{0,1:T(1,128)} %param.13) | copy-start | bytes 9220
  8.5 13.5 %copy-start.2 = (s32[1536]{0:T(1024)S(1)}, s32[1536]{0:T(1024)}, u32[]{:S(2)}) copy-start(s32[1536]{0:T(1024)} %param.17) | copy-start | bytes 18436
  12.7 20.9 %all-to-all-start = ((bf16[16,160,128]{2,1,0:T(8,128)(2,1)}), bf16[16,160,128]{2,1,0:T(8,128)(2,1)S(1)}, u32[]{:S(2)}, u32[]{:S(2)}) async-start(bf16[16,160,128]{2,1,0:T(8,128)(2,1)} %broadcast_in_dim.29), calls=%async_computation | async-start | bytes 1310720 | tf_op jit(solution)/shard_map/all_to_all | solution.py:525
  33.6 5.9 %copy-start.1 = (f32[56,1536]{1,0:T(8,128)S(1)}, f32[56,1536]{1,0:T(8,128)}, u32[]{:S(2)}) copy-start(f32[56,1536]{1,0:T(8,128)} %plan.3) | copy-start | bytes 1032196
  33.7 22.2 %all-to-all-start.1 = ((bf16[8,576,128]{2,1,0:T(8,128)(2,1)}), bf16[8,576,128]{2,1,0:T(8,128)(2,1)S(1)}, u32[]{:S(2)}, u32[]{:S(2)}) async-start(bf16[8,576,128]{2,1,0:T(8,128)(2,1)} %bitcast.16), calls=%async_computation.1 | async-start | bytes 2359296 | tf_op jit(solution)/shard_map/all_to_all | solution.py:525
  58.4 9.3 %collective-permute-start = (bf16[16,288,128]{2,1,0:T(8,128)(2,1)}, bf16[16,288,128]{2,1,0:T(8,128)(2,1)S(1)}, u32[]{:S(2)}, u32[]{:S(2)}) collective-permute-start(bf16[16,288,128]{2,1,0:T(8,128)(2,1)} %copy.23.x_ref), channel_id=1, source_target_pairs={{0,16},{16,0},{32,48},{48,32},{64,80},{80,64},{96,112},{112,96},{1... | collective-permute-start | bytes 3538952 | tf_op jit(solution)/shard_map/ppermute | solution.py:595
  59.4 26.3 %all-to-all-start.2 = ((bf16[16,288,128]{2,1,0:T(8,128)(2,1)}), bf16[16,288,128]{2,1,0:T(8,128)(2,1)S(1)}, u32[]{:S(2)}, u32[]{:S(2)}) async-start(bf16[16,288,128]{2,1,0:T(8,128)(2,1)} %copy.23.x_ref), calls=%async_computation.2 | async-start | bytes 2359296 | tf_op jit(solution)/shard_map/all_to_all | solution.py:525
  65.9 75.6 %all-gather.2.cloned.1.call-start = ((), (), s32[]{:S(2)}) async-start(), calls=%async_computation.6 | async-start | bytes 10616832 | tf_op jit(solution)/shard_map/all_gather | solution.py:608
  67.7 1.1 copy-start.5
  123.5 4.2 %collective-permute-start.1 = (f32[8,288,128]{2,1,0:T(8,128)}, f32[8,288,128]{2,1,0:T(8,128)S(1)}, u32[]{:S(2)}, u32[]{:S(2)}) collective-permute-start(f32[8,288,128]{2,1,0:T(8,128)} %get-tuple-element.34), channel_id=1, source_target_pairs={{0,16},{16,0},{32,48},{48,32},{64,80},{80,64},{96,112},{112,96},{1... | collective-permute-start | bytes 3538952 | tf_op jit(solution)/shard_map/ppermute | solution.py:610
  130.9 42.8 %all-to-all-start.3 = ((f32[16,288,128]{2,1,0:T(8,128)}), f32[16,288,128]{2,1,0:T(8,128)S(1)}, u32[]{:S(2)}, u32[]{:S(2)}) async-start(f32[16,288,128]{2,1,0:T(8,128)} %maximum_select_fusion.order_ref), calls=%async_computation.3 | async-start | bytes 4718592 | tf_op jit(solution)/shard_map/all_to_all | solution.py:525
  173.7 1.4 copy-start
Sparse Core Ops, SparseCore 0:
  87.7 53.6 all-gather.1

commit v2 on v1

--- a/solution.py
+++ b/solution.py
@@ -13,7 +13,7 @@
 HIGH = lax.Precision.HIGHEST
 BOTH = ("alpha", "beta")
 PAD = 8
-FIRST = 2
+FIRST = 1
 STEPS = 2
 WIDE = 32
 FEW = 16
@@ -99,7 +99,7 @@
     lax.fori_loop(0, blocks, build, 0)
 
 
-def plan_kernel(steps, width, tgt_ref, val_ref, cnt_ref, out_ref):
+def plan_kernel(steps, width, tgt_ref, val_ref, cnt_ref, out_ref, *row_refs):
     exc, length = tgt_ref.shape
     counts = cnt_ref[...]
     place = lax.broadcasted_iota(jnp.int32, (1, length), 1)
@@ -132,28 +132,49 @@
         over = jnp.sum(jnp.where(counts > k * steps, 1.0, 0.0), axis=1, keepdims=True)
         groups = ((over.astype(jnp.int32) + (width - 1)) // width).astype(F32)
         bounds = jnp.where(jnp.logical_and(lane == k, rows == 2), groups, bounds)
-    out_ref[0 : 3 * exc, :] = total[: 3 * exc]
-    out_ref[3 * exc :, :] = jnp.where(rows == 2, bounds, total[3 * exc :])
-
-
-def plan(targets, values, counts, steps, width):
+    tail = jnp.where(rows == 2, bounds, total[3 * exc :])
+    if not row_refs:
+        out_ref[0 : 3 * exc, :] = total[: 3 * exc]
+        out_ref[3 * exc :, :] = tail
+        return
+    (row_ref,) = row_refs
+    row_ref[...] = jnp.zeros_like(row_ref)
+    parts = length // 128
+    for ct in range(parts):
+        lanes = slice(ct * 128, (ct + 1) * 128)
+        for k in range(3):
+            row_ref[pl.ds(k * 64 + ct, exc, stride=parts), :] = total[
+                k * exc : (k + 1) * exc, lanes
+            ]
+        high_row = exc * parts + ct
+        row_ref[high_row : high_row + 1, :] = tail[0:1, lanes]
+        row_ref[64 + high_row : 65 + high_row, :] = tail[1:2, lanes]
+        bound_row = 64 + (exc + 1) * parts + ct
+        row_ref[bound_row : bound_row + 1, :] = tail[2:3, lanes]
+    out_ref[...] = row_ref[...].astype(BF16)
+
+
+def plan(targets, values, counts, steps, width, packed):
     exc, length = targets.shape
+    wanted = jax.ShapeDtypeStruct((3 * exc + 8, length), F32)
     return pl.pallas_call(
         functools.partial(plan_kernel, steps, width),
-        out_shape=jax.ShapeDtypeStruct((3 * exc + 8, length), F32),
+        out_shape=jax.ShapeDtypeStruct((256, 128), BF16) if packed else wanted,
+        scratch_shapes=[pltpu.VMEM((256, 128), F32)] if packed else [],
         compiler_params=pltpu.CompilerParams(vmem_limit_bytes=VMEM_LIMIT),
         name="plan",
     )(targets, values, counts[None, :])
 
 
-def beta_block(table_ref, tgt_ref, row_ref, w_ref, out_refs, wt_ref, acc_ref):
+def beta_block(table_ref, tgt_ref, row_ref, w_ref, out_refs, wt_ref, acc_ref, wide_ref):
     lanes = out_refs[0].shape[1] // 3
     exc = 16
     cols = 384
     slot = lax.broadcasted_iota(jnp.int32, (8, 128), 0) >> 1
+    wide_ref[...] = w_ref[0].astype(F32)
     for ct in range(3):
         turned = jnp.concatenate(
-            [w_ref[0, pl.ds(ct, exc, stride=3), :], jnp.zeros((128 - exc, 128), F32)], axis=0
+            [wide_ref[pl.ds(ct, exc, stride=3), :], jnp.zeros((128 - exc, 128), F32)], axis=0
         ).T
         for h in range(2):
             wt_ref[pl.ds(ct * 256 + h, 128, stride=2), :] = turned
@@ -199,84 +220,66 @@
             out_ref[0, pl.ds(ct, lanes, stride=3), :] = done[:lanes, ct * 128 : (ct + 1) * 128]
 
 
-def beta_first_kernel(
-    x_ref, y_ref, tgt_ref, row_ref, w_ref, own_ref, far_ref, table_ref, wt_ref, acc_ref, stage_ref
-):
-    @pl.when(pl.program_id(0) == 0)
-    def _():
-        build_table((x_ref, y_ref), table_ref, stage_ref)
-
-    beta_block(table_ref, tgt_ref, row_ref, w_ref, (own_ref, far_ref), wt_ref, acc_ref)
-
-
-def beta_rest_kernel(
-    table_ref, tgt_ref, row_ref, w_ref, old_own, old_far, own_ref, far_ref, wt_ref, acc_ref
-):
-    beta_block(table_ref, tgt_ref, row_ref, w_ref, (own_ref, far_ref), wt_ref, acc_ref)
-
-
-def list_specs(skip):
-    return [
-        pl.BlockSpec((8192,), lambda j: (j + skip,), memory_space=pltpu.SMEM),
-        pl.BlockSpec((1, 64, 128), lambda j: (j + skip, 0, 0)),
-        pl.BlockSpec((1, 48, 128), lambda j: (j + skip, 0, 0)),
-    ]
-
-
-def beta_params(blocks):
-    return dict(
+def table_kernel(x_ref, y_ref, table_ref, stage_ref):
+    build_table((x_ref, y_ref), table_ref, stage_ref)
+
+
+def slab_table(x2, y2):
+    nbeta, rows, _ = x2.shape
+    return pl.pallas_call(
+        table_kernel,
+        out_shape=jax.ShapeDtypeStruct((2 * nbeta * 384 + 2 * PAD, 128), F32),
+        in_specs=[pl.BlockSpec(memory_space=pltpu.VMEM)] * 2,
+        out_specs=pl.BlockSpec(memory_space=pltpu.VMEM),
+        scratch_shapes=[pltpu.VMEM((rows, 128), F32)],
+        compiler_params=pltpu.CompilerParams(vmem_limit_bytes=VMEM_LIMIT),
+        cost_estimate=pl.CostEstimate(flops=10**9, bytes_accessed=2**23, transcendentals=0),
+        name="slab_table",
+    )(x2, y2)
+
+
+def beta_kernel(side_ref, table_ref, tgt_ref, row_ref, w_ref, *refs):
+    own_ref, far_ref, wt_ref, acc_ref, wide_ref = refs[-5:]
+    beta_block(
+        table_ref, tgt_ref, row_ref, w_ref, (own_ref, far_ref), wt_ref, acc_ref, wide_ref
+    )
+
+
+def beta_term(side, table, numbers, heard, rows, skip, blocks, old):
+    half = numbers.shape[0]
+    nbeta = heard.shape[0]
+    near = pl.BlockSpec((1, rows, 128), lambda j, side: (side[0] * half + j + skip, 0, 0))
+    far = pl.BlockSpec((1, rows, 128), lambda j, side: (j + skip, 0, 0))
+    return pl.pallas_call(
+        beta_kernel,
+        out_shape=(
+            jax.ShapeDtypeStruct((nbeta, rows, 128), F32),
+            jax.ShapeDtypeStruct((half, rows, 128), F32),
+        ),
+        grid_spec=pltpu.PrefetchScalarGridSpec(
+            num_scalar_prefetch=1,
+            grid=(blocks,),
+            in_specs=[
+                pl.BlockSpec(table.shape, lambda j, side: (0, 0)),
+                pl.BlockSpec((8192,), lambda j, side: (j + skip,), memory_space=pltpu.SMEM),
+                pl.BlockSpec((1, 64, 128), lambda j, side: (j + skip, 0, 0)),
+                pl.BlockSpec((1, 64, 128), lambda j, side: (side[0] * half + j + skip, 2, 0)),
+            ]
+            + [pl.BlockSpec(memory_space=pl.ANY)] * len(old),
+            out_specs=(near, far),
+            scratch_shapes=[
+                pltpu.VMEM((768, 128), F32),
+                pltpu.VMEM((768, 128), F32),
+                pltpu.VMEM((64, 128), F32),
+            ],
+        ),
+        input_output_aliases={5: 0, 6: 1} if old else {},
         compiler_params=pltpu.CompilerParams(vmem_limit_bytes=VMEM_LIMIT),
         cost_estimate=pl.CostEstimate(
             flops=blocks * 8 * 10**8, bytes_accessed=blocks * 2**20, transcendentals=0
         ),
-    )
-
-
-def beta_first(x2, y2, numbers, weights, blocks):
-    nbeta, rows, _ = x2.shape
-    half = numbers.shape[0]
-    height = 2 * nbeta * 384 + 2 * PAD
-    piece = pl.BlockSpec((1, rows, 128), lambda j: (j, 0, 0))
-    slab = pl.BlockSpec((nbeta, rows, 128), lambda j: (0, 0, 0))
-    return pl.pallas_call(
-        beta_first_kernel,
-        out_shape=(
-            jax.ShapeDtypeStruct((half, rows, 128), F32),
-            jax.ShapeDtypeStruct((half, rows, 128), F32),
-            jax.ShapeDtypeStruct((height, 128), F32),
-        ),
-        grid=(blocks,),
-        in_specs=[slab, slab] + list_specs(0),
-        out_specs=(piece, piece, pl.BlockSpec((height, 128), lambda j: (0, 0))),
-        scratch_shapes=[
-            pltpu.VMEM((768, 128), F32),
-            pltpu.VMEM((768, 128), F32),
-            pltpu.VMEM((rows, 128), F32),
-        ],
-        name="beta_first",
-        **beta_params(blocks),
-    )(x2, y2, numbers.reshape(-1), numbers, weights)
-
-
-def beta_rest(table, numbers, weights, own, far, skip):
-    half, rows, _ = own.shape
-    piece = pl.BlockSpec((1, rows, 128), lambda j: (j + skip, 0, 0))
-    return pl.pallas_call(
-        beta_rest_kernel,
-        out_shape=(
-            jax.ShapeDtypeStruct(own.shape, F32),
-            jax.ShapeDtypeStruct(own.shape, F32),
-        ),
-        grid=(half - skip,),
-        in_specs=[pl.BlockSpec(table.shape, lambda j: (0, 0))]
-        + list_specs(skip)
-        + [pl.BlockSpec(memory_space=pl.ANY)] * 2,
-        out_specs=(piece, piece),
-        scratch_shapes=[pltpu.VMEM((768, 128), F32), pltpu.VMEM((768, 128), F32)],
-        input_output_aliases={4: 0, 5: 1},
-        name="beta_rest",
-        **beta_params(half - skip),
-    )(table, numbers.reshape(-1), numbers, weights, own, far)
+        name="beta_rest" if old else "beta_first",
+    )(side, table, numbers.reshape(-1), numbers, heard, *old)
 
 
 def alpha_kernel(
@@ -425,6 +428,8 @@
     return pl.pallas_call(
         functools.partial(merge_kernel, nalpha),
         out_shape=jax.ShapeDtypeStruct((devices, pieces, 128), BF16),
+        in_specs=[pl.BlockSpec(memory_space=pltpu.VMEM)] * 2,
+        out_specs=pl.BlockSpec(memory_space=pltpu.VMEM),
         compiler_params=pltpu.CompilerParams(vmem_limit_bytes=VMEM_LIMIT),
         name="merge",
     )(alpha, beta)
@@ -498,11 +503,12 @@
     rest = sigma - ratio * coef
     rho = jnp.sum(jnp.sum(rest * rest, axis=1, keepdims=True), axis=0, keepdims=True)
     lane = lax.broadcasted_iota(jnp.int32, (1, 128), 1)
-    part_ref[...] = jnp.where(
+    part = jnp.where(
         lane == 0,
         square,
         jnp.where(lane == 1, cross, jnp.where(lane == 2, rho, jnp.where(lane == 3, ratio, 0.0))),
     )
+    part_ref[...] = jnp.broadcast_to(part[None], part_ref.shape)
 
 
 def unpack(returned, key, labels, coef, transforms):
@@ -510,7 +516,7 @@
         unpack_kernel,
         out_shape=(
             jax.ShapeDtypeStruct(coef.shape, F32),
-            jax.ShapeDtypeStruct((1, 128), F32),
+            jax.ShapeDtypeStruct((returned.shape[0], 1, 128), F32),
         ),
         scratch_shapes=[
             pltpu.VMEM((returned.shape[0] * returned.shape[1], 128), F32),
@@ -548,22 +554,8 @@
     exc = alpha_targets.shape[0]
     pieces = capacity * width // 128
     labels = jnp.stack([conf_class, conf_tile[:, 0]])
-    bplan = plan(beta_targets, beta_values, beta_counts, STEPS, FEW)
-    zero = jnp.zeros((1, bplan.shape[1]), F32)
-    lists = jnp.concatenate(
-        [
-            bplan[:exc],
-            bplan[3 * exc : 3 * exc + 1],
-            zero,
-            bplan[exc : 2 * exc],
-            bplan[3 * exc + 1 : 3 * exc + 3],
-            bplan[2 * exc : 3 * exc],
-        ],
-        axis=0,
-    ).astype(BF16)
-    lists = lists.reshape(-1, 128)
-    lists = jnp.pad(lists, ((0, -lists.shape[0] % 16), (0, 0)))
-    aplan = plan(alpha_targets, alpha_values, alpha_counts, STEPS, WIDE)
+    lists = plan(beta_targets, beta_values, beta_counts, STEPS, FEW, True)
+    aplan = plan(alpha_targets, alpha_values, alpha_counts, STEPS, WIDE, False)
     anumbers = jnp.concatenate(
         [
             aplan[:exc] * 384.0 + aplan[exc : 2 * exc] * 3.0,
@@ -576,10 +568,8 @@
     aweights = aplan[2 * exc : 3 * exc]
 
     body_rows = nalpha * pieces
-    heard = exchange(jnp.broadcast_to(lists[None], (nbeta,) + lists.shape), "beta")
-    labels, lists = lax.optimization_barrier((labels, lists))
+    heard = lax.all_gather(lists, "beta", axis=0, tiled=False)
     outgoing, key = pack(csf_coef, labels, transforms, capacity)
-    outgoing, heard = lax.optimization_barrier((outgoing, heard))
     slab = exchange(outgoing.reshape(nalpha, nbeta * pieces, 128), "alpha")
     slab, anumbers, aweights = lax.optimization_barrier((slab, anumbers, aweights))
     x2 = (
@@ -587,39 +577,34 @@
         .transpose(1, 0, 2, 3)
         .reshape(nbeta, body_rows, 128)
     )
-    nrows = (exc + 2) * (bplan.shape[1] // 128)
-    wrows = exc * (bplan.shape[1] // 128)
     half = nbeta // 2
     side = lax.axis_index("alpha") % 2
     swap = [(i, i ^ 1) for i in range(nalpha)]
     y2 = lax.ppermute(x2, "alpha", swap)
+    btable = slab_table(x2, y2)
     mine = lax.dynamic_slice_in_dim(heard, side * half, half, axis=0)
-    high = mine[:, :nrows].astype(jnp.int32)
-    low = mine[:, nrows : 2 * nrows].astype(jnp.int32)
-    bnumbers = jnp.pad(high * 256 + low * 2, ((0, 0), (0, 64 - nrows), (0, 0)))
-    bweights = mine[:, 2 * nrows : 2 * nrows + wrows].astype(F32)
+    bnumbers = mine[:, :64].astype(jnp.int32) * 256 + mine[:, 64:128].astype(jnp.int32) * 2
+    sides = side.astype(jnp.int32)[None]
 
     got = exchange(x2, "beta")
-    near_a, far_a, btable = beta_first(x2, y2, bnumbers, bweights, FIRST)
-    got, btable = lax.optimization_barrier((got, btable))
+    early = beta_term(sides, btable, bnumbers, heard, body_rows, 0, FIRST, ())
+    got, bnumbers, early = lax.optimization_barrier((got, bnumbers, early))
     flat = (
         got.reshape(nbeta, nalpha, pieces, 128).transpose(1, 0, 2, 3).reshape(-1, 128)
     )
     table = lax.all_gather(flat, "alpha", axis=0, tiled=True)
-    near_b, far_b = beta_rest(btable, bnumbers, bweights, near_a, far_a, FIRST)
-    back = lax.ppermute(far_b, "alpha", swap)
-    beta_slab = jnp.where(
-        side == 0,
-        jnp.concatenate([near_b, back], axis=0),
-        jnp.concatenate([back, near_b], axis=0),
-    )
+    near, far = beta_term(
+        sides, btable, bnumbers, heard, body_rows, FIRST, half - FIRST, tuple(early)
+    )
+    back = lax.ppermute(far, "alpha", swap)
+    beta_slab = lax.dynamic_update_slice(near, back, ((1 - side) * half, 0, 0))
     beta_tile = exchange(beta_slab, "beta")
     own = (lax.axis_index("alpha") * rows_alpha).astype(jnp.int32)[None]
     partial = alpha_term(own, table, anumbers, aweights, det_diag, beta_slab)
     sigma_tile = merge(partial, beta_tile, nalpha, pieces)
     returned = exchange(sigma_tile, BOTH)
     sigma, part = unpack(returned, key, labels, csf_coef, transforms)
-    parts = exchange(jnp.broadcast_to(part[None], (devices, 1, 128)), BOTH)
+    parts = exchange(part, BOTH)
     residual, rms = finish(parts, sigma, csf_coef, ncsf * confs * devices)
     return (residual, rms[0, 0])
 

time: 237 us -> 234 us (0.987)
  waiting for transfers between devices: 26.1 us -> 20.9 us
  Pallas kernels: 106 us -> 110 us
  starting transfers between devices: 29.5 us -> 26.4 us
  blocking collectives: 42.1 us -> 45.1 us
    all_to_all x4 -> x3, starting transfers between devices: 27 us -> 18.7 us  [exchange(): return lax.all_to_all(x, axes, split_axis=0, concat_axis=0, tiled=True)]
    all_to_all x4 -> x3, waiting for transfers between devices: 18.7 us -> 12.1 us  [exchange(): return lax.all_to_all(x, axes, split_axis=0, concat_axis=0, tiled=True)]
    ppermute x1, starting transfers between devices: 1.29 us -> 6.68 us  [body(): back = lax.ppermute(far, 'alpha', swap)]
    pallas_call x2 -> x3, Pallas kernels: 52.7 us -> 56.7 us  [the longest x2 50 us: beta_term(): pl.pallas_call(beta_kernel, out_shape=(jax.ShapeDtypeStruct((nbeta, rows,...]
    select_n x1 -> x0, other arithmetic: 3.25 us -> none  [body(): jnp.where(side == 0, jnp.concatenate([near_b, back], axis=0), jnp.concate...]
    all_to_all x2, blocking collectives: 42.1 us -> 45.1 us  [exchange(): return lax.all_to_all(x, axes, split_axis=0, concat_axis=0, tiled=True)]
  transfers between devices with their start and end apart: 7 -> 7, of which waited for: 4 -> 5; matrix products, arithmetic and copies ran while one was open for 3% -> 5% of each run, Pallas kernels for 39% -> 41%
where the time goes in v2:
time: 234 us; the launch traced here: 233 us
  Pallas kernels  110 us (47%)
  blocking collectives  45.1 us (19%)
  starting transfers between devices  26.4 us (11%)
  waiting for transfers between devices  20.9 us (9%)
  between operations  14.1 us (6%)
  local copies, waits for them, and re-layouts  11.3 us (5%)
  other arithmetic  5.62 us (2%)
    pallas_call x2, Pallas kernels, beta_term(): pl.pallas_call(beta_kernel, out_shape=(jax.ShapeDtypeStruct((nbeta, rows,...  50 us
    all_to_all x2, blocking collectives, exchange(): return lax.all_to_all(x, axes, split_axis=0, concat_axis=0, tiled=True)  45.1 us
    pallas_call x1, Pallas kernels, alpha_term(): pl.pallas_call(alpha_kernel, out_shape=jax.ShapeDtypeStruct((rows * 3, 12...  28.5 us
    all_to_all x3, starting transfers between devices, exchange(): return lax.all_to_all(x, axes, split_axis=0, concat_axis=0, tiled=True)  18.7 us
    all_to_all x3, waiting for transfers between devices, exchange(): return lax.all_to_all(x, axes, split_axis=0, concat_axis=0, tiled=True)  12.1 us
    pallas_call x1, Pallas kernels, slab_table(): pl.pallas_call(table_kernel, out_shape=jax.ShapeDtypeStruct((2 * nbeta *...  6.72 us
    ppermute x1, starting transfers between devices, body(): back = lax.ppermute(far, 'alpha', swap)  6.68 us
    pallas_call x1, Pallas kernels, pack(): pl.pallas_call(functools.partial(pack_kernel, capacity), out_shape=(jax.S...  6.68 us
  transfers between devices with their start and end apart: 7, of which 5 were waited for; matrix products, arithmetic and copies ran while one was open for 5% of the time, Pallas kernels for 41%

profile of v2, /device:TPU:1, one launch (start us, length us, event | category | flops | bytes accessed | tf_op | source)
XLA Modules:
  0.0 233.1 jit_solution(10864188190839277010)
XLA Ops:
  7.2 0.0 all-gather.6.cloned.1.call-start
  7.2 1.2 broadcast_in_dim.14.cnt_ref
  8.5 1.9 plan.3
  10.4 0.0 all-gather.6.cloned.1.call-update
  10.4 0.7 stack.6
  11.1 1.3 pad_add_fusion.label_ref
  12.4 0.0 copy-start.2
  12.4 6.7 %pack.1 = (bf16[4608,128]{1,0:T(8,128)(2,1)}, s32[1,768]{1,0:T(1,128)}) custom-call(f32[42,768]{1,0:T(8,128)} %coef_ref.5, s32[2,768]{1,0:T(2,128)} %pad_add_fusion.label_ref, f32[6,42,256]{2,1,0:T(8,128)} %tr_ref.3), custom_call_target="tpu_custom_call" | custom-call | tf_op jit(solution)/shard_map/pack/pallas_call | solution.py:73
  19.1 5.8 %all-to-all-start = ((bf16[8,576,128]{2,1,0:T(8,128)(2,1)}), bf16[8,576,128]{2,1,0:T(8,128)(2,1)S(1)}, u32[]{:S(2)}, u32[]{:S(2)}) async-start(bf16[8,576,128]{2,1,0:T(8,128)(2,1)} %bitcast.23), calls=%async_computation | async-start | bytes 2359296 | tf_op jit(solution)/shard_map/all_to_all | solution.py:531
  24.8 0.0 copy-done.2
  24.9 0.6 broadcast_in_dim.13.cnt_ref
  25.4 4.4 %plan.2 = f32[56,1536]{1,0:T(8,128)} custom-call(s32[16,1536]{1,0:T(8,128)} %tgt_ref.2, bf16[16,1536]{1,0:T(8,128)(2,1)} %val_ref.2, s32[1,1536]{1,0:T(1,128)} %broadcast_in_dim.13.cnt_ref), custom_call_target="tpu_custom_call" | custom-call | tf_op jit(solution)/shard_map/plan/pallas_call | solution.py:160
  29.9 0.9 fusion.1
  30.8 1.7 fusion.2
  32.5 0.7 convert_element_type.14.tgt_ref
  33.1 8.1 %all-to-all-done = bf16[8,576,128]{2,1,0:T(8,128)(2,1)S(1)} async-done(((bf16[8,576,128]{2,1,0:T(8,128)(2,1)}), bf16[8,576,128]{2,1,0:T(8,128)(2,1)S(1)}, u32[]{:S(2)}, u32[]{:S(2)}) %all-to-all-start) | async-done | bytes 1179680 | tf_op jit(solution)/shard_map/all_to_all | solution.py:531
  41.2 0.8 copy.21
  42.0 0.5 copy.22
  42.5 1.3 copy.23.x_ref
  43.8 1.0 collective-permute-start
  44.8 7.8 %all-to-all-start.1 = ((bf16[16,288,128]{2,1,0:T(8,128)(2,1)}), bf16[16,288,128]{2,1,0:T(8,128)(2,1)S(1)}, u32[]{:S(2)}, u32[]{:S(2)}) async-start(bf16[16,288,128]{2,1,0:T(8,128)(2,1)} %copy.23.x_ref), calls=%async_computation.1 | async-start | bytes 2359296 | tf_op jit(solution)/shard_map/all_to_all | solution.py:531
  52.5 0.0 all-gather.4.cloned.1.call-start
  52.6 2.0 all-gather.6.cloned.1.call-done
  54.6 1.7 multiply_add_fusion.row_ref
  56.4 0.0 collective-permute-done.y_ref
  56.4 0.0 copy-start.1
  56.4 1.0 copy-done.1
  57.4 6.7 %slab_table.1.table_ref = f32[12304,128]{1,0:T(8,128)} custom-call(bf16[16,288,128]{2,1,0:T(8,128)(2,1)} %copy.23.x_ref, bf16[16,288,128]{2,1,0:T(8,128)(2,1)} %copy-done.1), custom_call_target="tpu_custom_call" | custom-call | flops 1000000000 | bytes 8388608 | tf_op jit(solution)/shard_map/slab_table/pallas_call | solution.py:229
  64.1 8.8 %beta_first.1 = (f32[16,288,128]{2,1,0:T(8,128)}, f32[8,288,128]{2,1,0:T(8,128)}) custom-call(s32[1]{0:T(128)} %bitcast.7.side_ref, f32[12304,128]{1,0:T(8,128)} %slab_table.1.table_ref, s32[65536]{0:T(1024)} %bitcast.18, s32[8,64,128]{2,1,0:T(8,128)} %multiply_add_fusion.row_ref, bf16[16,256,128]{2,1,0:T(8,128)(2,1)} %bitcast.21), custom_call_target="tpu_custom_call" | custom-call | flops 800000000 | bytes 1048576 | tf_op jit(solution)/shard_map/beta_first/pallas_call | solution.py:253
  73.0 0.0 all-to-all-done.1
  73.0 0.5 copy.26
  73.4 0.3 copy.27
  73.8 1.2 reshape.33
  74.9 0.0 all-gather.4.cloned.1.call-update
  75.0 41.2 %beta_rest.1 = (f32[16,288,128]{2,1,0:T(8,128)}, f32[8,288,128]{2,1,0:T(8,128)}) custom-call(s32[1]{0:T(128)} %bitcast.7.side_ref, f32[12304,128]{1,0:T(8,128)} %slab_table.1.table_ref, s32[65536]{0:T(1024)} %bitcast.19, s32[8,64,128]{2,1,0:T(8,128)} %multiply_add_fusion.row_ref, ...), custom_call_target="tpu_custom_call", output_to_operand_aliasing={{0}: (5, {}), {1}: (6, {})} | custom-call | flops 5600000000 | bytes 7340032 | tf_op jit(solution)/shard_map/beta_rest/pallas_call | solution.py:253
  116.2 6.7 %collective-permute-start.1 = (f32[8,288,128]{2,1,0:T(8,128)}, f32[8,288,128]{2,1,0:T(8,128)S(1)}, u32[]{:S(2)}, u32[]{:S(2)}) collective-permute-start(f32[8,288,128]{2,1,0:T(8,128)} %get-tuple-element.30), channel_id=1, source_target_pairs={{0,16},{16,0},{32,48},{48,32},{64,80},{80,64},{96,112},{112,96},{1... | collective-permute-start | bytes 3538952 | tf_op jit(solution)/shard_map/ppermute | solution.py:599
  122.8 3.1 %collective-permute-done.1 = f32[8,288,128]{2,1,0:T(8,128)S(1)} collective-permute-done((f32[8,288,128]{2,1,0:T(8,128)}, f32[8,288,128]{2,1,0:T(8,128)S(1)}, u32[]{:S(2)}, u32[]{:S(2)}) %collective-permute-start.1) | collective-permute-done | bytes 1179680 | tf_op jit(solution)/shard_map/ppermute | solution.py:599
  125.9 1.1 constant_dynamic-update-slice_fusion.order_ref
  127.0 5.1 %all-to-all-start.2 = ((f32[16,288,128]{2,1,0:T(8,128)}), f32[16,288,128]{2,1,0:T(8,128)S(1)}, u32[]{:S(2)}, u32[]{:S(2)}) async-start(f32[16,288,128]{2,1,0:T(8,128)} %constant_dynamic-update-slice_fusion.order_ref), calls=%async_computation.2 | async-start | bytes 4718592 | tf_op jit(solution)/shard_map/all_to_all | solution.py:531
  132.2 3.7 %all-gather.4.cloned.1.call-done.tbl_hbm = bf16[36864,128]{1,0:T(8,128)(2,1)} async-done(((bf16[4608,128]{1,0:T(8,128)(2,1)}), bf16[36864,128]{1,0:T(8,128)(2,1)}) %all-gather.4.cloned.1.call-update) | async-done | bytes 9437200 | tf_op jit(solution)/shard_map/all_gather | solution.py:595
  135.9 28.5 %alpha_term.1.alpha_ref = f32[4608,128]{1,0:T(8,128)} custom-call(s32[1]{0:T(128)} %bitcast.own_ref, bf16[36864,128]{1,0:T(8,128)(2,1)} %all-gather.4.cloned.1.call-done.tbl_hbm, s32[27648]{0:T(1024)} %convert_element_type.14.tgt_ref, f32[16,1536]{1,0:T(8,128)} %get-tuple-element.25.w_ref, f32[1536,384]{1,0:T(8,128)} %diag_ref.1, ...), custom_call_target="tpu_custom_call" | custom-call | flops 10000000000 | bytes 16777216 | tf_op jit(solution)/shard_map/alpha_term/pallas_call | solution.py:384
  164.3 4.0 %all-to-all-done.2.beta_ref = f32[16,288,128]{2,1,0:T(8,128)S(1)} async-done(((f32[16,288,128]{2,1,0:T(8,128)}), f32[16,288,128]{2,1,0:T(8,128)S(1)}, u32[]{:S(2)}, u32[]{:S(2)}) %all-to-all-start.2) | async-done | bytes 2359328 | tf_op jit(solution)/shard_map/all_to_all | solution.py:531
  168.3 1.4 copy-done
  169.8 3.8 %merge.1 = bf16[128,36,128]{2,1,0:T(8,128)(2,1)} custom-call(f32[4608,128]{1,0:T(8,128)} %alpha_term.1.alpha_ref, f32[16,288,128]{2,1,0:T(8,128)} %copy-done), custom_call_target="tpu_custom_call" | custom-call | tf_op jit(solution)/shard_map/merge/pallas_call | solution.py:428
  173.5 29.2 %all_to_all.25.r_ref = bf16[128,36,128]{2,1,0:T(8,128)(2,1)} all-to-all(bf16[128,36,128]{2,1,0:T(8,128)(2,1)} %merge.1), channel_id=1, replica_groups=mesh['alpha'=8,'beta'=16] {'alpha','beta'}, dimensions={0} | all-to-all | bytes 2359296 | tf_op jit(solution)/shard_map/all_to_all | solution.py:531
  202.7 5.7 %unpack.1 = (f32[42,768]{1,0:T(8,128)}, f32[128,1,128]{2,1,0:T(1,128)}) custom-call(bf16[128,36,128]{2,1,0:T(8,128)(2,1)} %all_to_all.25.r_ref, s32[1,768]{1,0:T(1,128)} %get-tuple-element.31.key_ref, s32[2,768]{1,0:T(2,128)} %pad_add_fusion.label_ref, f32[42,768]{1,0:T(8,128)} %coef_ref.5, f32[6,42,256]{2,1,0:T(8,128)} %tr_ref.3), custom_call_target="tpu_custom_call" | custom-call | tf_op jit(solution)/shard_map/unpack/pallas_call | solution.py:515
  208.4 15.9 %all_to_all.26.parts_ref = f32[128,1,128]{2,1,0:T(1,128)} all-to-all(f32[128,1,128]{2,1,0:T(1,128)} %get-tuple-element.32), channel_id=1, replica_groups=mesh['alpha'=8,'beta'=16] {'alpha','beta'}, dimensions={0} | all-to-all | bytes 131072 | tf_op jit(solution)/shard_map/all_to_all | solution.py:531
  224.4 1.9 finish.1
  (2 shorter events, 0.0 us)
Async XLA Ops:
  7.2 47.5 %all-gather.6.cloned.1.call-start = ((), (), s32[]{:S(2)}) async-start(), calls=%async_computation.6 | async-start | bytes 1114112 | tf_op jit(solution)/shard_map/all_gather | solution.py:571
  12.4 12.5 %copy-start.2 = (s32[1536]{0:T(1024)S(1)}, s32[1536]{0:T(1024)}, u32[]{:S(2)}) copy-start(s32[1536]{0:T(1024)} %param.17) | copy-start | bytes 18436
  19.1 22.2 %all-to-all-start = ((bf16[8,576,128]{2,1,0:T(8,128)(2,1)}), bf16[8,576,128]{2,1,0:T(8,128)(2,1)S(1)}, u32[]{:S(2)}, u32[]{:S(2)}) async-start(bf16[8,576,128]{2,1,0:T(8,128)(2,1)} %bitcast.23), calls=%async_computation | async-start | bytes 2359296 | tf_op jit(solution)/shard_map/all_to_all | solution.py:531
  43.8 12.6 %collective-permute-start = (bf16[16,288,128]{2,1,0:T(8,128)(2,1)}, bf16[16,288,128]{2,1,0:T(8,128)(2,1)S(1)}, u32[]{:S(2)}, u32[]{:S(2)}) collective-permute-start(bf16[16,288,128]{2,1,0:T(8,128)(2,1)} %copy.23.x_ref), channel_id=1, source_target_pairs={{0,16},{16,0},{32,48},{48,32},{64,80},{80,64},{96,112},{112,96},{1... | collective-permute-start | bytes 3538952 | tf_op jit(solution)/shard_map/ppermute | solution.py:583
  44.8 28.2 %all-to-all-start.1 = ((bf16[16,288,128]{2,1,0:T(8,128)(2,1)}), bf16[16,288,128]{2,1,0:T(8,128)(2,1)S(1)}, u32[]{:S(2)}, u32[]{:S(2)}) async-start(bf16[16,288,128]{2,1,0:T(8,128)(2,1)} %copy.23.x_ref), calls=%async_computation.1 | async-start | bytes 2359296 | tf_op jit(solution)/shard_map/all_to_all | solution.py:531
  52.5 83.3 %all-gather.4.cloned.1.call-start = ((), (), s32[]{:S(2)}) async-start(), calls=%async_computation.5 | async-start | bytes 10616832 | tf_op jit(solution)/shard_map/all_gather | solution.py:595
  56.4 1.0 copy-start.1
  116.2 9.8 %collective-permute-start.1 = (f32[8,288,128]{2,1,0:T(8,128)}, f32[8,288,128]{2,1,0:T(8,128)S(1)}, u32[]{:S(2)}, u32[]{:S(2)}) collective-permute-start(f32[8,288,128]{2,1,0:T(8,128)} %get-tuple-element.30), channel_id=1, source_target_pairs={{0,16},{16,0},{32,48},{48,32},{64,80},{80,64},{96,112},{112,96},{1... | collective-permute-start | bytes 3538952 | tf_op jit(solution)/shard_map/ppermute | solution.py:599
  127.0 41.3 %all-to-all-start.2 = ((f32[16,288,128]{2,1,0:T(8,128)}), f32[16,288,128]{2,1,0:T(8,128)S(1)}, u32[]{:S(2)}, u32[]{:S(2)}) async-start(f32[16,288,128]{2,1,0:T(8,128)} %constant_dynamic-update-slice_fusion.order_ref), calls=%async_computation.2 | async-start | bytes 4718592 | tf_op jit(solution)/shard_map/all_to_all | solution.py:531
  168.3 1.4 copy-start
Sparse Core Ops, SparseCore 0:
  10.5 44.0 all-gather.5
  75.1 60.7 all-gather.3

commit v3 on v2

--- a/solution.py
+++ b/solution.py
@@ -33,16 +33,16 @@
     return jnp.concatenate([value, jnp.zeros((fill, value.shape[1]), F32)], axis=0)
 
 
-def pack_kernel(capacity, coef_ref, label_ref, tr_ref, out_ref, key_ref, inter_ref):
+def pack_kernel(capacity, coef_ref, class_ref, tile_ref, tr_ref, out_ref, key_ref, inter_ref):
     confs = coef_ref.shape[1]
     ncls = tr_ref.shape[0]
     devices = confs * 3 // capacity
-    masked = stacked(padded(coef_ref), label_ref[0:1, :], ncls)
+    masked = stacked(padded(coef_ref), class_ref[...], ncls)
     trans = jnp.concatenate([padded(tr_ref, c) for c in range(ncls)], axis=0)
     dets = lax.dot_general(
         masked, trans, (((0,), (0,)), ((), ())), precision=HIGH, preferred_element_type=F32
     ).astype(BF16)
-    tile = label_ref[1:2, :]
+    tile = tile_ref[...]
     hit = lax.broadcasted_iota(jnp.int32, (devices, confs), 0) == tile
     before = lax.broadcasted_iota(jnp.int32, (confs, confs), 0) < lax.broadcasted_iota(
         jnp.int32, (confs, confs), 1
@@ -67,7 +67,7 @@
         out_ref[pl.ds(b * 2 * block, 2 * block), :] = inter_ref[...].astype(BF16)
 
 
-def pack(coef, labels, transforms, capacity):
+def pack(coef, classes, tiles, transforms, capacity):
     confs = coef.shape[1]
     rows = 2 * 3 * confs
     return pl.pallas_call(
@@ -79,7 +79,7 @@
         scratch_shapes=[pltpu.VMEM((512, 128), F32)],
         compiler_params=pltpu.CompilerParams(vmem_limit_bytes=VMEM_LIMIT),
         name="pack",
-    )(coef, labels, transforms)
+    )(coef, classes, tiles, transforms)
 
 
 def build_table(slab_refs, table_ref, stage_ref):
@@ -409,28 +409,28 @@
 
 
 def merge_kernel(nalpha, alpha_ref, beta_ref, out_ref):
-    nbeta = beta_ref.shape[0]
-    pieces = out_ref.shape[1]
+    devices, pieces, _ = out_ref.shape
+    nbeta = devices // nalpha
 
     def senders(beta_s, carry):
         for alpha_s in range(nalpha):
             p = alpha_s * nbeta + beta_s
+            q = beta_s * nalpha + alpha_s
             one = alpha_ref[pl.ds(p * pieces, pieces), :]
-            other = beta_ref[beta_s, alpha_s * pieces : (alpha_s + 1) * pieces, :]
+            other = beta_ref[pl.ds(q * pieces, pieces), :]
             out_ref[p] = (one + other).astype(BF16)
         return carry
 
     lax.fori_loop(0, nbeta, senders, 0)
 
 
-def merge(alpha, beta, nalpha, pieces):
-    devices = nalpha * beta.shape[0]
+def merge(alpha, beta, nalpha, devices):
     return pl.pallas_call(
         functools.partial(merge_kernel, nalpha),
-        out_shape=jax.ShapeDtypeStruct((devices, pieces, 128), BF16),
+        out_shape=jax.ShapeDtypeStruct((devices, alpha.shape[0] // devices, 128), BF16),
         in_specs=[pl.BlockSpec(memory_space=pltpu.VMEM)] * 2,
         out_specs=pl.BlockSpec(memory_space=pltpu.VMEM),
-        compiler_params=pltpu.CompilerParams(vmem_limit_bytes=VMEM_LIMIT),
+        compiler_params=pltpu.CompilerParams(vmem_limit_bytes=16 * 2**20),
         name="merge",
     )(alpha, beta)
 
@@ -458,7 +458,7 @@
 
 
 def unpack_kernel(
-    r_ref, key_ref, label_ref, coef_ref, tr_ref, sigma_ref, part_ref, stage_ref, half_ref
+    r_ref, key_ref, class_ref, coef_ref, tr_ref, sigma_ref, part_ref, stage_ref, half_ref
 ):
     devices, pieces, _ = r_ref.shape
     rows = devices * pieces // 2
@@ -467,11 +467,13 @@
     ncls = tr_ref.shape[0]
     tall = width + -width % 8
 
-    def spread(p, carry):
-        stage_ref[pl.ds(p * pieces, pieces), :] = r_ref[p].astype(F32)
+    def spread(i, carry):
+        for u in range(8):
+            p = i * 8 + u
+            stage_ref[pl.ds(p * pieces, pieces), :] = r_ref[p].astype(F32)
         return carry
 
-    lax.fori_loop(0, devices, spread, 0)
+    lax.fori_loop(0, devices // 8, spread, 0)
     for h in range(2):
         half_ref[:, h * 128 : (h + 1) * 128] = stage_ref[pl.ds(h, rows, stride=2), :].astype(BF16)
     key = key_ref[...]
@@ -494,7 +496,7 @@
     sigma = jnp.zeros((width, confs), F32)
     for c in range(ncls):
         part = products[c * tall : c * tall + width]
-        sigma = sigma + jnp.where(label_ref[0:1, :] == c, part, 0.0)
+        sigma = sigma + jnp.where(class_ref[...] == c, part, 0.0)
     coef = coef_ref[...]
     sigma_ref[...] = sigma
     square = jnp.sum(jnp.sum(coef * coef, axis=1, keepdims=True), axis=0, keepdims=True)
@@ -511,7 +513,7 @@
     part_ref[...] = jnp.broadcast_to(part[None], part_ref.shape)
 
 
-def unpack(returned, key, labels, coef, transforms):
+def unpack(returned, key, classes, coef, transforms):
     return pl.pallas_call(
         unpack_kernel,
         out_shape=(
@@ -524,7 +526,7 @@
         ],
         compiler_params=pltpu.CompilerParams(vmem_limit_bytes=VMEM_LIMIT),
         name="unpack",
-    )(returned, key, labels, coef, transforms)
+    )(returned, key, classes, coef, transforms)
 
 
 def exchange(x, axes):
@@ -553,7 +555,8 @@
     width = transforms.shape[2]
     exc = alpha_targets.shape[0]
     pieces = capacity * width // 128
-    labels = jnp.stack([conf_class, conf_tile[:, 0]])
+    classes = conf_class[None, :]
+    tiles = conf_tile.reshape(1, -1)
     lists = plan(beta_targets, beta_values, beta_counts, STEPS, FEW, True)
     aplan = plan(alpha_targets, alpha_values, alpha_counts, STEPS, WIDE, False)
     anumbers = jnp.concatenate(
@@ -569,7 +572,7 @@
 
     body_rows = nalpha * pieces
     heard = lax.all_gather(lists, "beta", axis=0, tiled=False)
-    outgoing, key = pack(csf_coef, labels, transforms, capacity)
+    outgoing, key = pack(csf_coef, classes, tiles, transforms, capacity)
     slab = exchange(outgoing.reshape(nalpha, nbeta * pieces, 128), "alpha")
     slab, anumbers, aweights = lax.optimization_barrier((slab, anumbers, aweights))
     x2 = (
@@ -600,10 +603,10 @@
     beta_slab = lax.dynamic_update_slice(near, back, ((1 - side) * half, 0, 0))
     beta_tile = exchange(beta_slab, "beta")
     own = (lax.axis_index("alpha") * rows_alpha).astype(jnp.int32)[None]
-    partial = alpha_term(own, table, anumbers, aweights, det_diag, beta_slab)
-    sigma_tile = merge(partial, beta_tile, nalpha, pieces)
+    partial = alpha_term(own, table, anumbers, aweights, det_diag, beta_slab[0, :8])
+    sigma_tile = merge(partial, beta_tile.reshape(-1, 128), nalpha, devices)
     returned = exchange(sigma_tile, BOTH)
-    sigma, part = unpack(returned, key, labels, csf_coef, transforms)
+    sigma, part = unpack(returned, key, classes, csf_coef, transforms)
     parts = exchange(part, BOTH)
     residual, rms = finish(parts, sigma, csf_coef, ncsf * confs * devices)
     return (residual, rms[0, 0])

time: 234 us -> 230 us (0.983)
  Pallas kernels: 110 us -> 106 us
    pallas_call x1, Pallas kernels: 3.79 us -> 0.36 us  [merge(): pl.pallas_call(functools.partial(merge_kernel, nalpha), out_shape=jax.Sha...]
  transfers between devices with their start and end apart: 7 -> 7, of which waited for: 5 -> 5; matrix products, arithmetic and copies ran while one was open for 5% -> 5% of each run, Pallas kernels for 41% -> 42%
where the time goes in v3:
time: 230 us; the launch traced here: 229 us
  Pallas kernels  106 us (46%)
  blocking collectives  44.9 us (20%)
  starting transfers between devices  26.3 us (11%)
  waiting for transfers between devices  20.3 us (9%)
  between operations  14.1 us (6%)
  local copies, waits for them, and re-layouts  13.4 us (6%)
  other arithmetic  4.35 us (2%)
    pallas_call x2, Pallas kernels, beta_term(): pl.pallas_call(beta_kernel, out_shape=(jax.ShapeDtypeStruct((nbeta, rows,...  50 us
    all_to_all x2, blocking collectives, exchange(): return lax.all_to_all(x, axes, split_axis=0, concat_axis=0, tiled=True)  44.9 us
    pallas_call x1, Pallas kernels, alpha_term(): pl.pallas_call(alpha_kernel, out_shape=jax.ShapeDtypeStruct((rows * 3, 12...  28.5 us
    all_to_all x3, starting transfers between devices, exchange(): return lax.all_to_all(x, axes, split_axis=0, concat_axis=0, tiled=True)  17.9 us
    all_to_all x3, waiting for transfers between devices, exchange(): return lax.all_to_all(x, axes, split_axis=0, concat_axis=0, tiled=True)  12.1 us
    ppermute x1, starting transfers between devices, body(): back = lax.ppermute(far, 'alpha', swap)  7.36 us
    pallas_call x1, Pallas kernels, slab_table(): pl.pallas_call(table_kernel, out_shape=jax.ShapeDtypeStruct((2 * nbeta *...  6.72 us
    pallas_call x1, Pallas kernels, pack(): pl.pallas_call(functools.partial(pack_kernel, capacity), out_shape=(jax.S...  6.68 us
  transfers between devices with their start and end apart: 7, of which 5 were waited for; matrix products, arithmetic and copies ran while one was open for 5% of the time, Pallas kernels for 42%

profile of v3, /device:TPU:1, one launch (start us, length us, event | category | flops | bytes accessed | tf_op | source)
XLA Modules:
  0.0 229.0 jit_solution(8253237313942587982)
XLA Ops:
  7.2 0.0 all-gather.6.cloned.1.call-start
  7.2 1.2 broadcast_in_dim.18.cnt_ref
  8.5 1.9 plan.3
  10.4 0.0 all-gather.6.cloned.1.call-update
  10.4 1.3 broadcast_in_dim.16.class_ref
  11.7 0.0 copy-start.2
  11.7 6.7 %pack.1 = (bf16[4608,128]{1,0:T(8,128)(2,1)}, s32[1,768]{1,0:T(1,128)}) custom-call(f32[42,768]{1,0:T(8,128)} %coef_ref.5, s32[1,768]{1,0:T(1,128)} %broadcast_in_dim.16.class_ref, s32[1,768]{1,0:T(1,128)} %bitcast.28, f32[6,42,256]{2,1,0:T(8,128)} %tr_ref.3), custom_call_target="tpu_custom_call" | custom-call | tf_op jit(solution)/shard_map/pack/pallas_call | solution.py:73
  18.4 5.8 %all-to-all-start = ((bf16[8,576,128]{2,1,0:T(8,128)(2,1)}), bf16[8,576,128]{2,1,0:T(8,128)(2,1)S(1)}, u32[]{:S(2)}, u32[]{:S(2)}) async-start(bf16[8,576,128]{2,1,0:T(8,128)(2,1)} %bitcast.27), calls=%async_computation | async-start | bytes 2359296 | tf_op jit(solution)/shard_map/all_to_all | solution.py:533
  24.2 0.0 copy-done.2
  24.2 0.6 broadcast_in_dim.17.cnt_ref
  24.8 4.4 %plan.2 = f32[56,1536]{1,0:T(8,128)} custom-call(s32[16,1536]{1,0:T(8,128)} %tgt_ref.2, bf16[16,1536]{1,0:T(8,128)(2,1)} %val_ref.2, s32[1,1536]{1,0:T(1,128)} %broadcast_in_dim.17.cnt_ref), custom_call_target="tpu_custom_call" | custom-call | tf_op jit(solution)/shard_map/plan/pallas_call | solution.py:160
  29.2 0.9 fusion.1
  30.1 1.7 fusion.2
  31.8 0.7 convert_element_type.14.tgt_ref
  32.4 8.1 %all-to-all-done = bf16[8,576,128]{2,1,0:T(8,128)(2,1)S(1)} async-done(((bf16[8,576,128]{2,1,0:T(8,128)(2,1)}), bf16[8,576,128]{2,1,0:T(8,128)(2,1)S(1)}, u32[]{:S(2)}, u32[]{:S(2)}) %all-to-all-start) | async-done | bytes 1179680 | tf_op jit(solution)/shard_map/all_to_all | solution.py:533
  40.5 0.8 copy.21
  41.3 0.5 copy.22
  41.8 1.3 copy.23.x_ref
  43.1 1.0 collective-permute-start
  44.1 7.8 %all-to-all-start.1 = ((bf16[16,288,128]{2,1,0:T(8,128)(2,1)}), bf16[16,288,128]{2,1,0:T(8,128)(2,1)S(1)}, u32[]{:S(2)}, u32[]{:S(2)}) async-start(bf16[16,288,128]{2,1,0:T(8,128)(2,1)} %copy.23.x_ref), calls=%async_computation.1 | async-start | bytes 2359296 | tf_op jit(solution)/shard_map/all_to_all | solution.py:533
  51.9 0.0 all-gather.4.cloned.1.call-start
  51.9 2.7 %all-gather.6.cloned.1.call-done = bf16[4096,128]{1,0:T(8,128)(2,1)} async-done(((bf16[256,128]{1,0:T(8,128)(2,1)}), bf16[4096,128]{1,0:T(8,128)(2,1)}) %all-gather.6.cloned.1.call-update) | async-done | bytes 1048592 | tf_op jit(solution)/shard_map/all_gather | solution.py:574
  54.6 1.7 multiply_add_fusion.row_ref
  56.4 0.0 collective-permute-done.y_ref
  56.4 0.0 copy-start.1
  56.4 1.0 copy-done.1
  57.4 6.7 %slab_table.1.table_ref = f32[12304,128]{1,0:T(8,128)} custom-call(bf16[16,288,128]{2,1,0:T(8,128)(2,1)} %copy.23.x_ref, bf16[16,288,128]{2,1,0:T(8,128)(2,1)} %copy-done.1), custom_call_target="tpu_custom_call" | custom-call | flops 1000000000 | bytes 8388608 | tf_op jit(solution)/shard_map/slab_table/pallas_call | solution.py:229
  64.1 8.8 %beta_first.1 = (f32[16,288,128]{2,1,0:T(8,128)}, f32[8,288,128]{2,1,0:T(8,128)}) custom-call(s32[1]{0:T(128)} %bitcast.7.side_ref, f32[12304,128]{1,0:T(8,128)} %slab_table.1.table_ref, s32[65536]{0:T(1024)} %bitcast.22, s32[8,64,128]{2,1,0:T(8,128)} %multiply_add_fusion.row_ref, bf16[16,256,128]{2,1,0:T(8,128)(2,1)} %bitcast.25), custom_call_target="tpu_custom_call" | custom-call | flops 800000000 | bytes 1048576 | tf_op jit(solution)/shard_map/beta_first/pallas_call | solution.py:253
  73.0 0.0 all-to-all-done.1
  73.0 0.5 copy.26
  73.4 0.3 copy.27
  73.8 1.2 reshape.40
  74.9 0.0 all-gather.4.cloned.1.call-update
  75.0 41.2 %beta_rest.1 = (f32[16,288,128]{2,1,0:T(8,128)}, f32[8,288,128]{2,1,0:T(8,128)}) custom-call(s32[1]{0:T(128)} %bitcast.7.side_ref, f32[12304,128]{1,0:T(8,128)} %slab_table.1.table_ref, s32[65536]{0:T(1024)} %bitcast.23, s32[8,64,128]{2,1,0:T(8,128)} %multiply_add_fusion.row_ref, ...), custom_call_target="tpu_custom_call", output_to_operand_aliasing={{0}: (5, {}), {1}: (6, {})} | custom-call | flops 5600000000 | bytes 7340032 | tf_op jit(solution)/shard_map/beta_rest/pallas_call | solution.py:253
  116.2 7.4 %collective-permute-start.1 = (f32[8,288,128]{2,1,0:T(8,128)}, f32[8,288,128]{2,1,0:T(8,128)S(1)}, u32[]{:S(2)}, u32[]{:S(2)}) collective-permute-start(f32[8,288,128]{2,1,0:T(8,128)} %get-tuple-element.30), channel_id=1, source_target_pairs={{0,16},{16,0},{32,48},{48,32},{64,80},{80,64},{96,112},{112,96},{1... | collective-permute-start | bytes 3538952 | tf_op jit(solution)/shard_map/ppermute | solution.py:602
  123.5 3.1 %collective-permute-done.1 = f32[8,288,128]{2,1,0:T(8,128)S(1)} collective-permute-done((f32[8,288,128]{2,1,0:T(8,128)}, f32[8,288,128]{2,1,0:T(8,128)S(1)}, u32[]{:S(2)}, u32[]{:S(2)}) %collective-permute-start.1) | collective-permute-done | bytes 1179680 | tf_op jit(solution)/shard_map/ppermute | solution.py:602
  126.6 1.1 constant_dynamic-update-slice_fusion
  127.7 4.3 %all-to-all-start.2 = ((f32[16,288,128]{2,1,0:T(8,128)}), f32[16,288,128]{2,1,0:T(8,128)S(1)}, u32[]{:S(2)}, u32[]{:S(2)}) async-start(f32[16,288,128]{2,1,0:T(8,128)} %constant_dynamic-update-slice_fusion), calls=%async_computation.2 | async-start | bytes 4718592 | tf_op jit(solution)/shard_map/all_to_all | solution.py:533
  132.1 1.3 slice_bitcast_fusion.order_ref
  133.4 2.4 %all-gather.4.cloned.1.call-done.tbl_hbm = bf16[36864,128]{1,0:T(8,128)(2,1)} async-done(((bf16[4608,128]{1,0:T(8,128)(2,1)}), bf16[36864,128]{1,0:T(8,128)(2,1)}) %all-gather.4.cloned.1.call-update) | async-done | bytes 9437200 | tf_op jit(solution)/shard_map/all_gather | solution.py:598
  135.7 28.5 %alpha_term.1.alpha_ref = f32[4608,128]{1,0:T(8,128)} custom-call(s32[1]{0:T(128)} %bitcast.own_ref, bf16[36864,128]{1,0:T(8,128)(2,1)} %all-gather.4.cloned.1.call-done.tbl_hbm, s32[27648]{0:T(1024)} %convert_element_type.14.tgt_ref, f32[16,1536]{1,0:T(8,128)} %get-tuple-element.25.w_ref, f32[1536,384]{1,0:T(8,128)} %diag_ref.1, ...), custom_call_target="tpu_custom_call" | custom-call | flops 10000000000 | bytes 16777216 | tf_op jit(solution)/shard_map/alpha_term/pallas_call | solution.py:384
  164.2 4.0 %all-to-all-done.2 = f32[16,288,128]{2,1,0:T(8,128)S(1)} async-done(((f32[16,288,128]{2,1,0:T(8,128)}), f32[16,288,128]{2,1,0:T(8,128)S(1)}, u32[]{:S(2)}, u32[]{:S(2)}) %all-to-all-start.2) | async-done | bytes 2359328 | tf_op jit(solution)/shard_map/all_to_all | solution.py:533
  168.2 1.7 copy-done
  169.9 0.4 merge.1
  170.2 29.0 %all_to_all.25.r_ref = bf16[128,36,128]{2,1,0:T(8,128)(2,1)} all-to-all(bf16[128,36,128]{2,1,0:T(8,128)(2,1)S(1)} %merge.1), channel_id=1, replica_groups=mesh['alpha'=8,'beta'=16] {'alpha','beta'}, dimensions={0} | all-to-all | bytes 2359296 | tf_op jit(solution)/shard_map/all_to_all | solution.py:533
  199.2 5.1 %unpack.1 = (f32[42,768]{1,0:T(8,128)}, f32[128,1,128]{2,1,0:T(1,128)}) custom-call(bf16[128,36,128]{2,1,0:T(8,128)(2,1)} %all_to_all.25.r_ref, s32[1,768]{1,0:T(1,128)} %get-tuple-element.31.key_ref, s32[1,768]{1,0:T(1,128)} %broadcast_in_dim.16.class_ref, f32[42,768]{1,0:T(8,128)} %coef_ref.5, f32[6,42,256]{2,1,0:T(8,128)} %tr_ref.3), custom_call_target="tpu_custom_call" | custom-call | tf_op jit(solution)/shard_map/unpack/pallas_call | solution.py:517
  204.3 15.9 %all_to_all.26.parts_ref = f32[128,1,128]{2,1,0:T(1,128)} all-to-all(f32[128,1,128]{2,1,0:T(1,128)} %get-tuple-element.32), channel_id=1, replica_groups=mesh['alpha'=8,'beta'=16] {'alpha','beta'}, dimensions={0} | all-to-all | bytes 131072 | tf_op jit(solution)/shard_map/all_to_all | solution.py:533
  220.2 1.9 finish.1
  (2 shorter events, 0.0 us)
Async XLA Ops:
  7.2 47.5 %all-gather.6.cloned.1.call-start = ((), (), s32[]{:S(2)}) async-start(), calls=%async_computation.6 | async-start | bytes 1114112 | tf_op jit(solution)/shard_map/all_gather | solution.py:574
  11.7 12.5 %copy-start.2 = (s32[1536]{0:T(1024)S(1)}, s32[1536]{0:T(1024)}, u32[]{:S(2)}) copy-start(s32[1536]{0:T(1024)} %param.17) | copy-start | bytes 18436
  18.4 22.2 %all-to-all-start = ((bf16[8,576,128]{2,1,0:T(8,128)(2,1)}), bf16[8,576,128]{2,1,0:T(8,128)(2,1)S(1)}, u32[]{:S(2)}, u32[]{:S(2)}) async-start(bf16[8,576,128]{2,1,0:T(8,128)(2,1)} %bitcast.27), calls=%async_computation | async-start | bytes 2359296 | tf_op jit(solution)/shard_map/all_to_all | solution.py:533
  43.1 13.3 %collective-permute-start = (bf16[16,288,128]{2,1,0:T(8,128)(2,1)}, bf16[16,288,128]{2,1,0:T(8,128)(2,1)S(1)}, u32[]{:S(2)}, u32[]{:S(2)}) collective-permute-start(bf16[16,288,128]{2,1,0:T(8,128)(2,1)} %copy.23.x_ref), channel_id=1, source_target_pairs={{0,16},{16,0},{32,48},{48,32},{64,80},{80,64},{96,112},{112,96},{1... | collective-permute-start | bytes 3538952 | tf_op jit(solution)/shard_map/ppermute | solution.py:586
  44.1 28.9 %all-to-all-start.1 = ((bf16[16,288,128]{2,1,0:T(8,128)(2,1)}), bf16[16,288,128]{2,1,0:T(8,128)(2,1)S(1)}, u32[]{:S(2)}, u32[]{:S(2)}) async-start(bf16[16,288,128]{2,1,0:T(8,128)(2,1)} %copy.23.x_ref), calls=%async_computation.1 | async-start | bytes 2359296 | tf_op jit(solution)/shard_map/all_to_all | solution.py:533
  51.9 83.9 %all-gather.4.cloned.1.call-start = ((), (), s32[]{:S(2)}) async-start(), calls=%async_computation.5 | async-start | bytes 10616832 | tf_op jit(solution)/shard_map/all_gather | solution.py:598
  56.4 1.0 copy-start.1
  116.2 10.5 %collective-permute-start.1 = (f32[8,288,128]{2,1,0:T(8,128)}, f32[8,288,128]{2,1,0:T(8,128)S(1)}, u32[]{:S(2)}, u32[]{:S(2)}) collective-permute-start(f32[8,288,128]{2,1,0:T(8,128)} %get-tuple-element.30), channel_id=1, source_target_pairs={{0,16},{16,0},{32,48},{48,32},{64,80},{80,64},{96,112},{112,96},{1... | collective-permute-start | bytes 3538952 | tf_op jit(solution)/shard_map/ppermute | solution.py:602
  127.7 40.5 %all-to-all-start.2 = ((f32[16,288,128]{2,1,0:T(8,128)}), f32[16,288,128]{2,1,0:T(8,128)S(1)}, u32[]{:S(2)}, u32[]{:S(2)}) async-start(f32[16,288,128]{2,1,0:T(8,128)} %constant_dynamic-update-slice_fusion), calls=%async_computation.2 | async-start | bytes 4718592 | tf_op jit(solution)/shard_map/all_to_all | solution.py:533
  168.2 1.7 copy-start
Sparse Core Ops, SparseCore 0:
  10.5 44.0 all-gather.5
  75.1 60.6 all-gather.3
